TPU v7x, 256 devices: a whole 4x4x8 slice. The times are simulated.
256 devices in a mesh: loop: 16 (over z, x_lo), row: 4 (over x_hi, core), col: 4 (over y).
Axes of the slice: x: 4 (x_hi: 2, x_lo: 2; x = x_hi * 2 + x_lo), y: 4, z: 8, core: 2. Of those that a mesh axis runs over, the one named last changes fastest.
Arguments:
- interval_blocks: bfloat16 [16, 4, 2048, 2048], P('loop', None, 'row', 'col'), may hold values from -0.15625 to 0.15625
- interval_pivots: int32 [16, 3, 2048], P('loop'), may hold values from 0 to 2047, each once within a row
- boundary_pivots: int32 [16, 2048], replicated, may hold values from 0 to 2047, each once within a row
- interval_residuals: bfloat16 [16, 4, 2048], P('loop', None, ('row', 'col')), may hold values from -0.23925781 to 0.23925781
Outputs:
- reduced_block: bfloat16 [16, 2048, 2048], P('loop', 'row', 'col')
- reduced_rhs: float32 [16, 2048], P('loop', ('row', 'col'))
Inputs may be any that keep to these rules, and one draw needn't show every extreme that they name: Each row of interval_pivots is a permutation of 0 to 2047. Each row of boundary_pivots is a permutation of 0 to 2047.
All inputs are finite; a program needn't handle non-finite values.
Results may differ from a plain program's by a relative error of at most 0.018.
Values may be sent and summed in bfloat16 or wider, within the bound.
A program may use at most 64 MiB of HBM per device.

v0:
```python
import jax
import jax.numpy as jnp
from jax import lax
from jax.sharding import PartitionSpec as P


def from_behind(value, axis, by):
    devices = lax.axis_size(axis)
    return lax.ppermute(value, axis, [(i, (i + by) % devices) for i in range(devices)])


def compose(left_block, right_block, right_vector, pivots, added):
    column_panel = lax.all_gather(right_block, "row", axis=0, tiled=True)
    full_vector = lax.all_gather(right_vector, ("row", "col"), axis=0, tiled=True)
    permuted = jnp.take(column_panel, pivots, axis=0)
    moved = jnp.take(full_vector, pivots, axis=0)
    segment = lax.all_gather(left_block, "col", axis=1, tiled=True)
    product = jnp.dot(segment, permuted, preferred_element_type=jnp.float32)
    applied = jnp.dot(segment, moved, preferred_element_type=jnp.float32)
    share_size = added.shape[0]
    own_part = lax.dynamic_slice_in_dim(applied, lax.axis_index("col") * share_size, share_size, 0)
    return (product, own_part + added.astype(jnp.float32))


def shards(interval_blocks, interval_pivots, boundary_pivots, interval_residuals):
    blocks = interval_blocks[0]
    pivot_rows = interval_pivots[0]
    residuals = interval_residuals[0]
    matrix = blocks[0]
    vector = residuals[0]
    for interval in range(1, blocks.shape[0]):
        product, applied = compose(
            blocks[interval], matrix, vector, pivot_rows[interval - 1], residuals[interval]
        )
        matrix = product.astype(jnp.bfloat16)
        vector = applied.astype(jnp.bfloat16)
    position = lax.axis_index("loop")
    count_loop = lax.axis_size("loop")
    own_pivots = lax.dynamic_index_in_dim(boundary_pivots, position, 0, keepdims=False)
    back_pivots = lax.dynamic_index_in_dim(
        boundary_pivots, (position + count_loop - 1) % count_loop, 0, keepdims=False
    )
    earlier, earlier_vector = from_behind((matrix, vector), "loop", 1)
    product, applied = compose(matrix, earlier, earlier_vector, own_pivots, vector)
    halved = product.astype(jnp.bfloat16)
    halved_vector = applied.astype(jnp.bfloat16)
    distant, distant_vector = from_behind((halved, halved_vector), "loop", 2)
    reduced, reduced_vector = compose(halved, distant, distant_vector, back_pivots, halved_vector)
    return (reduced.astype(jnp.bfloat16)[None], reduced_vector[None])


def solution(mesh):
    placed = (
        P("loop", None, "row", "col"),
        P("loop", None, None),
        P(),
        P("loop", None, ("row", "col")),
    )
    return jax.shard_map(
        shards,
        mesh=mesh,
        in_specs=placed,
        out_specs=(P("loop", "row", "col"), P("loop", ("row", "col"))),
        check_vma=False,
    )
```

profile of v0, /device:TPU:1, one launch (start us, length us, event | category | flops | bytes accessed | tf_op | source)
XLA Modules:
  0.0 391.1 jit_solution(15672747446238209155)
XLA Ops:
  10.9 32.7 %all-gather.4 = bf16[1,1,2048]{2,1,0:T(2,128)(2,1)S(1)} all-gather(bf16[1,1,128]{2,1,0:T(2,128)(2,1)S(1)} %slice.51), channel_id=6, replica_groups=mesh['loop'=16,'row'=4,'col'=4] {'row','col'}, dimensions={2}, use_global_device_ids=true | all-gather | bytes 4352 | tf_op jit(solution)/shard_map/all_gather | solution.py:14
  43.7 13.1 %gather_fusion.5 = bf16[2048]{0:T(1024)(128)(2,1)S(1)} fusion(bf16[2048]{0:T(1024)(128)(2,1)S(1)} %reduce, s32[2048]{0:T(1024)S(1)} %fusion.68), kind=kCustom, calls=%fused_computation.1.clone | custom fusion | bytes 16384 | tf_op jit(solution)/shard_map/jit(_take)/gather | solution.py:16
  56.8 9.5 %gather_fusion = bf16[2048,512]{1,0:T(8,128)(2,1)S(1)} fusion(bf16[2048,512]{1,0:T(8,128)(2,1)} %bitcast.80, s32[2048]{0:T(1024)S(1)} %fusion.68), kind=kCustom, calls=%fused_computation.clone | custom fusion | bytes 4202496 | tf_op jit(solution)/shard_map/jit(_take)/gather | solution.py:15
  66.4 11.8 %all-gather.34.cloned.1.call-done = bf16[1,1,512,2048]{3,2,1,0:T(8,128)(2,1)} async-done(((bf16[1,1,512,512]{3,2,1,0:T(8,128)(2,1)}), bf16[1,1,512,2048]{3,2,1,0:T(8,128)(2,1)}) %all-gather.34.cloned.1.call-update) | async-done | bytes 2097168 | tf_op jit(solution)/shard_map/all_gather | solution.py:17
  78.1 4.1 %fusion.55 = bf16[512,512]{0,1:T(8,128)(2,1)} fusion(bf16[1,1,512,2048]{3,2,1,0:T(8,128)(2,1)} %all-gather.34.cloned.1.call-done, bf16[2048,512]{1,0:T(8,128)(2,1)S(1)} %gather_fusion, pred[2048]{0:T(1024)(128)(4,1)S(1)} %get-tuple-element.13), kind=kOutput, calls=%fused_computation.41 | convolution fusion | flops 1075052544 | bytes 4720640 | tf_op jit(solution)/shard_map/dot_general | solution.py:18
  85.2 29.6 %all-gather.5 = bf16[16,1,128]{2,1,0:T(2,128)(2,1)S(1)} all-gather(bf16[1,1,128]{2,1,0:T(2,128)(2,1)S(1)} %fusion.77), channel_id=1, replica_groups=mesh['loop'=16,'row'=4,'col'=4] {'row','col'}, dimensions={0}, use_global_device_ids=true | all-gather | bytes 4352 | tf_op jit(solution)/shard_map/all_gather | solution.py:14
  114.9 13.1 %gather_fusion.6 = bf16[2048]{0:T(1024)(128)(2,1)S(1)} fusion(bf16[2048]{0:T(1024)(128)(2,1)S(1)} %bitcast.77, s32[2048]{0:T(1024)S(1)} %fusion.69), kind=kCustom, calls=%fused_computation.6.clone | custom fusion | bytes 16384 | tf_op jit(solution)/shard_map/jit(_take)/gather | solution.py:16
  130.9 9.2 %gather_fusion.1 = bf16[2048,512]{1,0:T(8,128)(2,1)} fusion(bf16[2048,512]{1,0:T(8,128)(2,1)S(1)} %copy.8, s32[2048]{0:T(1024)S(1)} %fusion.69), kind=kCustom, calls=%fused_computation.2.clone | custom fusion | bytes 4202496 | tf_op jit(solution)/shard_map/jit(_take)/gather | solution.py:15
  140.1 6.1 %all-gather.36.cloned.1.call-done = bf16[1,1,512,2048]{3,2,1,0:T(8,128)(2,1)} async-done(((bf16[1,1,512,512]{3,2,1,0:T(8,128)(2,1)}), bf16[1,1,512,2048]{3,2,1,0:T(8,128)(2,1)}) %all-gather.36.cloned.1.call-update) | async-done | bytes 2097168 | tf_op jit(solution)/shard_map/all_gather | solution.py:17
  146.2 4.8 %fusion.50 = bf16[512,512]{0,1:T(8,128)(2,1)} fusion(bf16[1,1,512,2048]{3,2,1,0:T(8,128)(2,1)} %all-gather.36.cloned.1.call-done, bf16[2048,512]{1,0:T(8,128)(2,1)} %gather_fusion.1, pred[2048]{0:T(1024)(128)(4,1)S(1)} %get-tuple-element.11), kind=kOutput, calls=%fused_computation.40 | convolution fusion | flops 1075052544 | bytes 4720640 | tf_op jit(solution)/shard_map/dot_general | solution.py:18
  152.4 29.6 %all-gather.6 = bf16[16,1,128]{2,1,0:T(2,128)(2,1)S(1)} all-gather(bf16[1,1,128]{2,1,0:T(2,128)(2,1)S(1)} %fusion.75), channel_id=1, replica_groups=mesh['loop'=16,'row'=4,'col'=4] {'row','col'}, dimensions={0}, use_global_device_ids=true | all-gather | bytes 4352 | tf_op jit(solution)/shard_map/all_gather | solution.py:14
  182.1 13.1 %gather_fusion.7 = bf16[2048]{0:T(1024)(128)(2,1)S(1)} fusion(bf16[2048]{0:T(1024)(128)(2,1)S(1)} %bitcast.78, s32[2048]{0:T(1024)S(1)} %fusion.70), kind=kCustom, calls=%fused_computation.7.clone | custom fusion | bytes 16384 | tf_op jit(solution)/shard_map/jit(_take)/gather | solution.py:16
  198.1 9.2 %gather_fusion.2 = bf16[2048,512]{1,0:T(8,128)(2,1)} fusion(bf16[2048,512]{1,0:T(8,128)(2,1)S(1)} %copy.9, s32[2048]{0:T(1024)S(1)} %fusion.70), kind=kCustom, calls=%fused_computation.3.clone | custom fusion | bytes 4202496 | tf_op jit(solution)/shard_map/jit(_take)/gather | solution.py:15
  207.3 7.7 %all-gather.38.cloned.1.call-done = bf16[1,1,512,2048]{3,2,1,0:T(8,128)(2,1)} async-done(((bf16[1,1,512,512]{3,2,1,0:T(8,128)(2,1)}), bf16[1,1,512,2048]{3,2,1,0:T(8,128)(2,1)}) %all-gather.38.cloned.1.call-update) | async-done | bytes 2097168 | tf_op jit(solution)/shard_map/all_gather | solution.py:17
  220.3 14.4 %collective-permute-done = bf16[512,512]{0,1:T(8,128)(2,1)S(1)} collective-permute-done((bf16[512,512]{0,1:T(8,128)(2,1)S(1)}, bf16[512,512]{0,1:T(8,128)(2,1)S(1)}, u32[]{:S(2)}, u32[]{:S(2)}) %collective-permute-start) | collective-permute-done | bytes 524320 | tf_op jit(solution)/shard_map/ppermute | solution.py:9
  238.2 4.5 %collective-permute-done.2 = bf16[128]{0:T(256)(128)(2,1)S(1)} collective-permute-done((bf16[128]{0:T(256)(128)(2,1)S(1)}, bf16[128]{0:T(256)(128)(2,1)S(1)}, u32[]{:S(2)}, u32[]{:S(2)}) %collective-permute-start.2) | collective-permute-done | bytes 288 | tf_op jit(solution)/shard_map/ppermute | solution.py:9
  242.7 29.2 %all-gather.7 = bf16[16,1,128]{2,1,0:T(2,128)(2,1)S(1)} all-gather(bf16[1,1,128]{2,1,0:T(2,128)(2,1)S(1)} %bitcast.97), channel_id=1, replica_groups=mesh['loop'=16,'row'=4,'col'=4] {'row','col'}, dimensions={0}, use_global_device_ids=true | all-gather | bytes 4352 | tf_op jit(solution)/shard_map/all_gather | solution.py:14
  271.9 13.1 %gather_fusion.8 = bf16[2048]{0:T(1024)(128)(2,1)S(1)} fusion(bf16[2048]{0:T(1024)(128)(2,1)S(1)} %bitcast.79, s32[2048]{0:T(1024)S(1)} %fusion.71), kind=kCustom, calls=%fused_computation.8.clone | custom fusion | bytes 16384 | tf_op jit(solution)/shard_map/jit(_take)/gather | solution.py:16
  287.9 9.2 %gather_fusion.3 = bf16[2048,512]{1,0:T(8,128)(2,1)} fusion(bf16[2048,512]{1,0:T(8,128)(2,1)S(1)} %copy.10, s32[2048]{0:T(1024)S(1)} %fusion.71), kind=kCustom, calls=%fused_computation.4.clone | custom fusion | bytes 4202496 | tf_op jit(solution)/shard_map/jit(_take)/gather | solution.py:15
  300.4 4.5 %fusion.24 = bf16[512,512]{1,0:T(8,128)(2,1)} fusion(bf16[512,2048]{0,1:T(8,128)(2,1)} %all-gather.24.cloned.1.call-done, bf16[2048,512]{1,0:T(8,128)(2,1)} %gather_fusion.3, pred[2048]{0:T(1024)(128)(4,1)S(1)} %get-tuple-element.7), kind=kOutput, calls=%fused_computation.34 | convolution fusion | flops 1075052544 | bytes 4720640 | tf_op jit(solution)/shard_map/dot_general | solution.py:18
  306.3 12.0 %collective-permute-done.1 = bf16[512,512]{1,0:T(8,128)(2,1)S(1)} collective-permute-done((bf16[512,512]{1,0:T(8,128)(2,1)}, bf16[512,512]{1,0:T(8,128)(2,1)S(1)}, u32[]{:S(2)}, u32[]{:S(2)}) %collective-permute-start.1) | collective-permute-done | bytes 524320 | tf_op jit(solution)/shard_map/ppermute | solution.py:9
  323.7 31.0 %all-gather.8 = bf16[16,1,128]{2,1,0:T(2,128)(2,1)S(1)} all-gather(bf16[1,1,128]{2,1,0:T(2,128)(2,1)S(1)} %bitcast.96), channel_id=1, replica_groups=mesh['loop'=16,'row'=4,'col'=4] {'row','col'}, dimensions={0}, use_global_device_ids=true | all-gather | bytes 4352 | tf_op jit(solution)/shard_map/all_gather | solution.py:14
  354.8 13.1 %gather_fusion.9 = bf16[2048]{0:T(1024)(128)(2,1)S(1)} fusion(bf16[2048]{0:T(1024)(128)(2,1)S(1)} %bitcast.76, s32[2048]{0:T(1024)S(1)} %fusion.72), kind=kCustom, calls=%fused_computation.9.clone | custom fusion | bytes 16384 | tf_op jit(solution)/shard_map/jit(_take)/gather | solution.py:16
  371.1 9.4 %gather_fusion.4 = bf16[2048,512]{1,0:T(8,128)(2,1)S(1)} fusion(bf16[2048,512]{1,0:T(8,128)(2,1)} %all-gather.30.cloned.1.call-done, s32[2048]{0:T(1024)S(1)} %fusion.72), kind=kCustom, calls=%fused_computation.5.clone | custom fusion | bytes 4202496 | tf_op jit(solution)/shard_map/jit(_take)/gather | solution.py:15
  (87 shorter events, 42.7 us)
Async XLA Ops:
  7.2 3.7 copy-start.7
  7.2 36.5 %copy-start.6 = (s32[1,3,2048]{2,0,1:T(1,128)S(1)}, s32[1,3,2048]{2,0,1:T(1,128)}, u32[]{:S(2)}) copy-start(s32[1,3,2048]{2,0,1:T(1,128)} %param.9) | copy-start | bytes 73732
  7.2 49.6 %all-gather.32.cloned.1.call-start = ((), (), s32[]{:S(2)}) async-start(), calls=%async_computation.6 | async-start | bytes 2621440 | tf_op jit(solution)/shard_map/all_gather | solution.py:13
  10.1 68.0 %all-gather.34.cloned.1.call-start = ((), (), s32[]{:S(2)}) async-start(), calls=%async_computation.7 | async-start | bytes 2621440 | tf_op jit(solution)/shard_map/all_gather | solution.py:17
  10.9 117.1 %all-gather.20.cloned.1.call-start = ((), (), s32[]{:S(2)}) async-start(), calls=%async_computation | async-start | bytes 2621440 | tf_op jit(solution)/shard_map/all_gather | solution.py:13
  82.2 63.9 %all-gather.36.cloned.1.call-start = ((), (), s32[]{:S(2)}) async-start(), calls=%async_computation.8 | async-start | bytes 2621440 | tf_op jit(solution)/shard_map/all_gather | solution.py:17
  82.8 112.4 %all-gather.22.cloned.1.call-start = ((), (), s32[]{:S(2)}) async-start(), calls=%async_computation.1 | async-start | bytes 2621440 | tf_op jit(solution)/shard_map/all_gather | solution.py:13
  146.2 5.5 %copy-start.2 = (bf16[1,1,512,2048]{3,2,1,0:T(8,128)(2,1)S(1)}, bf16[1,1,512,2048]{3,2,1,0:T(8,128)(2,1)}, u32[]{:S(2)}) copy-start(bf16[1,1,512,2048]{3,2,1,0:T(8,128)(2,1)} %all-gather.36.cloned.1.call-done) | copy-start | bytes 6291460
  151.0 63.9 %all-gather.38.cloned.1.call-start = ((), (), s32[]{:S(2)}) async-start(), calls=%async_computation.9 | async-start | bytes 2621440 | tf_op jit(solution)/shard_map/all_gather | solution.py:17
  151.6 133.4 %all-gather.26.cloned.1.call-start = ((), (), s32[]{:S(2)}) async-start(), calls=%async_computation.3 | async-start | bytes 2621440 | tf_op jit(solution)/shard_map/all_gather | solution.py:13
  215.0 22.3 %copy-start.1 = (bf16[1,1,512,2048]{3,2,1,0:T(8,128)(2,1)S(1)}, bf16[1,1,512,2048]{3,2,1,0:T(8,128)(2,1)}, u32[]{:S(2)}) copy-start(bf16[1,1,512,2048]{3,2,1,0:T(8,128)(2,1)} %all-gather.38.cloned.1.call-done) | copy-start | bytes 6291460
  219.0 16.6 %copy-start.3 = (bf16[512,512]{0,1:T(8,128)(2,1)}, bf16[512,512]{0,1:T(8,128)(2,1)S(1)}, u32[]{:S(2)}) copy-start(bf16[512,512]{0,1:T(8,128)(2,1)S(1)} %fusion.45) | copy-start | bytes 1572868
  219.0 15.7 %collective-permute-start = (bf16[512,512]{0,1:T(8,128)(2,1)S(1)}, bf16[512,512]{0,1:T(8,128)(2,1)S(1)}, u32[]{:S(2)}, u32[]{:S(2)}) collective-permute-start(bf16[512,512]{0,1:T(8,128)(2,1)S(1)} %fusion.45), channel_id=1, source_target_pairs={{0,16},{16,32},{32,48},{48,64},{64,80},{80,96},{96,112},{112,128},... | collective-permute-start | bytes 1572872 | tf_op jit(solution)/shard_map/ppermute | solution.py:9
  234.7 0.8 copy-start.4
  235.5 64.9 %all-gather.24.cloned.1.call-start = ((), (), s32[]{:S(2)}) async-start(), calls=%async_computation.2 | async-start | bytes 2621440 | tf_op jit(solution)/shard_map/all_gather | solution.py:17
  236.3 131.7 %all-gather.28.cloned.1.call-start = ((), (), s32[]{:S(2)}) async-start(), calls=%async_computation.4 | async-start | bytes 2621440 | tf_op jit(solution)/shard_map/all_gather | solution.py:17
  238.0 4.7 %collective-permute-start.2 = (bf16[128]{0:T(256)(128)(2,1)S(1)}, bf16[128]{0:T(256)(128)(2,1)S(1)}, u32[]{:S(2)}, u32[]{:S(2)}) collective-permute-start(bf16[128]{0:T(256)(128)(2,1)S(1)} %fusion.73), channel_id=1, source_target_pairs={{0,16},{16,32},{32,48},{48,64},{64,80},{80,96},{96,112},{112,128},... | collective-permute-start | bytes 776 | tf_op jit(solution)/shard_map/ppermute | solution.py:9
  300.4 18.8 %copy-start = (bf16[512,2048]{0,1:T(8,128)(2,1)S(1)}, bf16[512,2048]{0,1:T(8,128)(2,1)}, u32[]{:S(2)}) copy-start(bf16[512,2048]{0,1:T(8,128)(2,1)} %all-gather.24.cloned.1.call-done) | copy-start | bytes 6291460
  304.9 66.2 %all-gather.30.cloned.1.call-start = ((), (), s32[]{:S(2)}) async-start(), calls=%async_computation.5 | async-start | bytes 2621440 | tf_op jit(solution)/shard_map/all_gather | solution.py:13
  305.0 13.3 %collective-permute-start.1 = (bf16[512,512]{1,0:T(8,128)(2,1)}, bf16[512,512]{1,0:T(8,128)(2,1)S(1)}, u32[]{:S(2)}, u32[]{:S(2)}) collective-permute-start(bf16[512,512]{1,0:T(8,128)(2,1)} %fusion.24), channel_id=1, source_target_pairs={{0,32},{16,48},{32,64},{48,80},{64,96},{80,112},{96,128},{112,144}... | collective-permute-start | bytes 1572872 | tf_op jit(solution)/shard_map/ppermute | solution.py:9
  318.3 0.8 copy-start.5
  319.6 4.1 %collective-permute-start.3 = (bf16[128]{0:T(256)(128)(2,1)S(1)}, bf16[128]{0:T(256)(128)(2,1)S(1)}, u32[]{:S(2)}, u32[]{:S(2)}) collective-permute-start(bf16[128]{0:T(256)(128)(2,1)S(1)} %add_convert_fusion), channel_id=1, source_target_pairs={{0,32},{16,48},{32,64},{48,80},{64,96},{80,112},{96,128},{112,144}... | collective-permute-start | bytes 776 | tf_op jit(solution)/shard_map/ppermute | solution.py:9
Sparse Core Ops, SparseCore 0:
  10.4 33.3 all-gather.31
  45.6 32.4 all-gather.33
  82.3 29.6 all-gather.19
  113.7 32.4 all-gather.35
  151.2 29.5 all-gather.21
  182.5 32.4 all-gather.37
  235.7 29.7 all-gather.25
  267.9 32.4 all-gather.23
  305.0 34.7 all-gather.27
  341.5 29.6 all-gather.29
where the time goes:
time: 395 us; the launch traced here: 391 us
  blocking collectives  152 us (38%)
  local copies, waits for them, and re-layouts  126 us (32%)
  waiting for transfers between devices  65.9 us (17%)
  matrix products  27.3 us (7%)
  between operations  14.5 us (4%)
  starting transfers between devices  4.16 us (1%)
    all_gather x5, blocking collectives, compose(): lax.all_gather(right_vector, ('row', 'col'), axis=0, tiled=True)  152 us
    gather x5, local copies, waits for them, and re-layouts, compose(): moved = jnp.take(full_vector, pivots, axis=0)  65.4 us
    gather x5, local copies, waits for them, and re-layouts, compose(): permuted = jnp.take(column_panel, pivots, axis=0)  46.5 us
    ppermute x4, waiting for transfers between devices, from_behind(): lax.ppermute(value, axis, [(i, (i + by) % devices) for i in range(devices)])  34 us
    all_gather x5, waiting for transfers between devices, compose(): segment = lax.all_gather(left_block, 'col', axis=1, tiled=True)  28.9 us
    dot_general x5, matrix products, compose(): product = jnp.dot(segment, permuted, preferred_element_type=jnp.float32)  21.1 us
    all_gather x3, local copies, waits for them, and re-layouts, compose(): column_panel = lax.all_gather(right_block, 'row', axis=0, tiled=True)  8.63 us
  transfers between devices with their start and end apart: 14, of which 9 were waited for; matrix products, arithmetic and copies ran while one was open for 31% of the time, Pallas kernels for 0%

commit v1 on v0

v1 whole, which is shorter than its diff:
```python
import jax
import jax.numpy as jnp
from jax import lax
from jax.experimental import pallas as pl
from jax.experimental.pallas import tpu as pltpu
from jax.sharding import PartitionSpec as P

MESH = pl.DeviceIdType.MESH
BF, F32 = jnp.bfloat16, jnp.float32
NT = (((1,), (1,)), ((), ()))

ITEMS = (("F", 0), ("S", 0), ("F", 1), ("W", 0), ("S", 1), ("W", 1))
AHEAD = 3


def body(w_ref, ipiv_ref, bpiv_ref, res_ref, out_ref, rhs_ref, gath, own_vec, panel, perm, hot, gsend, gbuf, rbuf, gs_sem, gr_sem, ys_sem,
         yr_sem, ps_sem, pr_sem):
    loop, row, col = lax.axis_index("loop"), lax.axis_index("row"), lax.axis_index("col")
    n_loop, n_row, n_col = lax.axis_size("loop"), lax.axis_size("row"), lax.axis_size("col")
    nb = w_ref.shape[1]
    half, quarter = nb // 2, nb // 4
    share = res_ref.shape[1]

    def at(dloop=0, row_=None, dcol=0):
        return {
            "loop": lax.rem(loop + dloop + n_loop, n_loop),
            "row": row if row_ is None else row_,
            "col": lax.rem(col + dcol + n_col, n_col),
        }

    sibling = row + 1 - 2 * lax.rem(row, 2)
    across = lax.rem(row + 2, n_row)
    across_sibling = lax.rem(sibling + 2, n_row)
    slot_rows = (row, sibling, across, across_sibling)
    slot_cols = (col, lax.rem(col + n_col - 1, n_col), lax.rem(col + 2, n_col), lax.rem(col + 1, n_col))

    sends = []

    def send(src, dst, ssem, rsem, dev):
        copy = pltpu.make_async_remote_copy(
            src_ref=src, dst_ref=dst, send_sem=ssem, recv_sem=rsem, device_id=dev, device_id_type=MESH
        )
        copy.start()
        sends.append(copy)

    def arrived(dst, rsem):
        pltpu.make_async_remote_copy(
            src_ref=dst, dst_ref=dst, send_sem=rsem, recv_sem=rsem, device_id=at(), device_id_type=MESH
        ).wait_recv()

    def own_block(s):
        return w_ref.at[s + 1] if s < 3 else gath.at[s, 0]

    def item_refs(s, k, direction):
        kind, h = ITEMS[k]
        first = h * half + (0 if direction == 0 else quarter)
        second = h * half + (quarter if direction == 0 else 0)
        near = 1 if direction == 0 else 3
        if kind == "W":
            return gath.at[s, near, pl.ds(first, quarter)], gath.at[s, 2, pl.ds(first, quarter)]
        rows = first if kind == "F" else second
        return own_block(s).at[pl.ds(rows, quarter)], gath.at[s, near, pl.ds(rows, quarter)]

    def y_issue(s, k):
        for direction in (0, 1):
            src, dst = item_refs(s, k, direction)
            send(src, dst, ys_sem.at[s, k, direction], yr_sem.at[s, k, direction], at(dcol=1 if direction == 0 else -1))

    def y_recv(s, k):
        for direction in (0, 1):
            _, dst = item_refs(s, k, direction)
            arrived(dst, yr_sem.at[s, k, direction])
        s2, k2 = (s, k + AHEAD) if k + AHEAD < 6 else (s + 1, k + AHEAD - 6)
        if s2 < 3 or (s2 < 5 and s2 == s):
            y_issue(s2, k2)

    chunks = (pl.ds(0, half), pl.ds(half, half), pl.ds(nb, 16))

    def p_own(t, k):
        if t < 3:
            return panel.at[t, 0, chunks[k]]
        if k == 2:
            return own_vec.at[t - 3]
        return gath.at[t, 0, chunks[k]]

    def p_send(t, k, src, slot, dev):
        send(src, panel.at[t, slot, chunks[k]], ps_sem.at[t, slot, k], pr_sem.at[t, slot, k], dev)

    def p_recv(t, slot, k):
        arrived(panel.at[t, slot, chunks[k]], pr_sem.at[t, slot, k])

    def p_start(t, k):
        src = p_own(t, k)
        if t < 3:
            p_send(t, k, src, 1, at(row_=sibling))
            p_send(t, k, src, 2, at(row_=across))
        elif t == 3:
            p_send(t, k, src, 0, at(dloop=1))
            p_send(t, k, src, 2, at(dloop=1, row_=across))
        else:
            p_send(t, k, src, 0, at(dloop=2))

    def p_forward(t, k):
        if t >= 3:
            p_recv(t, 0, k)
            p_send(t, k, panel.at[t, 0, chunks[k]], 1, at(row_=sibling))
        if t == 4:
            p_send(t, k, panel.at[t, 0, chunks[k]], 2, at(row_=across))

    def p_forward_far(t, k):
        p_recv(t, 2, k)
        p_send(t, k, panel.at[t, 2, chunks[k]], 3, at(row_=sibling))

    def p_join(t, ks):
        for k in ks:
            p_recv(t, 1, k)
            p_recv(t, 3, k)

    def pivots(s, d):
        cols = pl.ds(pl.multiple_of(slot_cols[d] * nb, nb), nb)
        if s < 3:
            return ipiv_ref[pl.ds(s, 1), cols]
        return bpiv_ref[pl.ds(lax.rem(loop + n_loop - (s - 3), n_loop), 1), cols]

    def make_hot(s, d):
        q = pivots(s, d)
        for slot in range(4):
            iota = lax.broadcasted_iota(jnp.int32, (nb, nb), 0)
            hot[d, slot] = jnp.where(iota == q - slot_rows[slot] * nb, 1.0, 0.0).astype(BF)

    def permute(s, h, d, first=False):
        rows = pl.ds(h * half, half)
        left = (own_block(s) if d == 0 else gath.at[s, d])[rows, :]

        def one(slot, carry):
            moved = lax.dot_general(left, hot[d, slot], NT, preferred_element_type=F32).astype(BF)
            if first:
                perm[slot, rows, :] = moved
            else:
                perm[slot, rows, :] += moved
            return carry

        lax.fori_loop(0, 4, one, 0)

    def product(t, h):
        rows = pl.ds(h * half, half)
        total = jnp.dot(perm[0, rows, :], panel[t, 0, :nb, :], preferred_element_type=F32)
        for slot in range(1, 4):
            total += jnp.dot(perm[slot, rows, :], panel[t, slot, :nb, :], preferred_element_type=F32)
        return total

    def applied(t):
        total = lax.dot_general(panel[t, 0, nb:, :], perm[0], NT, preferred_element_type=F32)
        for slot in range(1, 4):
            total += lax.dot_general(panel[t, slot, nb:, :], perm[slot], NT, preferred_element_type=F32)
        return total

    def finish(s, h):
        rows = pl.ds(h * half, half)
        value = product(s, h).astype(BF)
        if s < 2:
            panel[s + 1, 0, rows, :] = value
        elif s < 4:
            gath[s + 1, 0, rows, :] = value
        else:
            out_ref[rows, :] = value

    def finish_vector(s):
        value = applied(s)
        if s < 3:
            value = (value + gbuf[pl.ds(s + 1, 1), :]).astype(BF)
        else:
            value = value + own_vec[s - 3].astype(F32)
        if s < 2:
            panel[s + 1, 0, nb:, :] = value
        elif s < 4:
            own_vec[s - 2] = value.astype(BF)
        else:
            rbuf[...] = value[:8, :]
            rhs_ref[...] = rbuf[pl.ds(0, 1), pl.ds(pl.multiple_of(col * share, share), share)]

    barrier = pltpu.get_barrier_semaphore()
    partners = (
        at(dcol=1), at(dcol=-1), at(dcol=2), at(row_=sibling), at(row_=across),
        at(dloop=1), at(dloop=-1), at(dloop=1, row_=across), at(dloop=-1, row_=across), at(dloop=2), at(dloop=-2),
    )
    for partner in partners:
        pl.semaphore_signal(barrier, inc=1, device_id=partner, device_id_type=MESH)
    panel[0, 0, :nb, :] = w_ref[0]
    own_cols = pl.ds(pl.multiple_of(col * share, share), share)
    gsend[...] = jnp.zeros_like(gsend)
    gsend[pl.ds(0, 4), pl.ds(0, share)] = res_ref[...].astype(F32)
    gbuf[:, own_cols] = gsend[:, pl.ds(0, share)]
    pl.semaphore_wait(barrier, len(partners))

    for k in range(AHEAD):
        y_issue(0, k)
    for k in (0, 1):
        p_start(0, k)
    for i, dcol in enumerate((1, -1, 2)):
        send(gsend.at[:, pl.ds(0, share)], gbuf.at[:, own_cols], gs_sem.at[i], gr_sem.at[i], at(dcol=dcol))
    make_hot(0, 0)
    permute(0, 0, 0, True)
    permute(0, 1, 0, True)
    make_hot(0, 1)
    make_hot(0, 3)
    for i, dcol in enumerate((-1, 1, 2)):
        arrived(gbuf.at[:, pl.ds(pl.multiple_of(lax.rem(col + dcol + n_col, n_col) * share, share), share)], gr_sem.at[i])
    panel[0, 0, nb:, :] = jnp.broadcast_to(gbuf[pl.ds(0, 1), :], (16, nb)).astype(BF)
    p_start(0, 2)

    for s in range(5):
        y_recv(s, 0)
        y_recv(s, 1)
        permute(s, 0, 1)
        permute(s, 0, 3)
        if s == 0:
            make_hot(0, 2)
        if s >= 3:
            p_forward(s, 0)
        if s < 4:
            p_forward_far(s, 0)
        y_recv(s, 2)
        y_recv(s, 3)
        permute(s, 0, 2)
        if s < 3:
            p_forward_far(s, 1)
            p_forward_far(s, 2)
            p_join(s, (0, 1, 2))
            finish(s, 0)
            p_start(s + 1, 0)
            if s == 2:
                y_issue(3, 0)
                y_issue(3, 1)
        y_recv(s, 4)
        permute(s, 1, 1)
        permute(s, 1, 3)
        if s >= 3:
            if s == 4:
                p_forward_far(s, 0)
            for k in (1, 2):
                p_forward(s, k)
                p_forward_far(s, k)
            p_join(s, (0, 1, 2))
            finish(s, 0)
            if s == 3:
                p_start(4, 0)
                y_issue(4, 0)
                y_issue(4, 1)
        y_recv(s, 5)
        permute(s, 1, 2)
        finish(s, 1)
        if s < 4:
            p_start(s + 1, 1)
            if s >= 2:
                y_issue(s + 1, 2)
        finish_vector(s)
        if s < 4:
            p_start(s + 1, 2)
            for d in (0, 1, 3, 2):
                make_hot(s + 1, d)
                if d == 0:
                    permute(s + 1, 0, 0, True)
                    permute(s + 1, 1, 0, True)
    for copy in sends:
        copy.wait_send()


def shards(interval_blocks, interval_pivots, boundary_pivots, interval_residuals):
    blocks, pivots, residuals = interval_blocks[0], interval_pivots[0], interval_residuals[0]
    nb, share = blocks.shape[1], residuals.shape[1]
    vmem = pl.BlockSpec(memory_space=pltpu.VMEM)
    reduced, rhs = pl.pallas_call(
        body,
        out_shape=(jax.ShapeDtypeStruct((nb, nb), BF), jax.ShapeDtypeStruct((1, share), F32)),
        in_specs=[vmem] * 4,
        out_specs=(vmem, vmem),
        scratch_shapes=[
            pltpu.VMEM((5, 4, nb, nb), BF),
            pltpu.VMEM((2, 16, nb), BF),
            pltpu.VMEM((5, 4, nb + 16, nb), BF),
            pltpu.VMEM((4, nb, nb), BF),
            pltpu.VMEM((4, 4, nb, nb), BF),
            pltpu.VMEM((8, nb), F32),
            pltpu.VMEM((8, nb), F32),
            pltpu.VMEM((8, nb), F32),
            pltpu.SemaphoreType.DMA((3,)),
            pltpu.SemaphoreType.DMA((3,)),
            pltpu.SemaphoreType.DMA((5, 6, 2)),
            pltpu.SemaphoreType.DMA((5, 6, 2)),
            pltpu.SemaphoreType.DMA((5, 4, 3)),
            pltpu.SemaphoreType.DMA((5, 4, 3)),
        ],
        compiler_params=pltpu.CompilerParams(
            collective_id=0, has_side_effects=True, vmem_limit_bytes=60 * 2**20
        ),
        name="newton",
    )(blocks, pivots, boundary_pivots, residuals)
    return reduced[None], rhs


def solution(mesh):
    placed = (
        P("loop", None, "row", "col"),
        P("loop", None, None),
        P(),
        P("loop", None, ("row", "col")),
    )
    return jax.shard_map(
        shards,
        mesh=mesh,
        in_specs=placed,
        out_specs=(P("loop", "row", "col"), P("loop", ("row", "col"))),
        check_vma=False,
    )
```

time: 395 us -> 140 us (0.35); the launches traced: 391 us -> 140 us
  blocking collectives: 152 us -> 0 us
  Pallas kernels: 0 us -> 135 us
  local copies, waits for them, and re-layouts: 126 us -> 4.34 us
  waiting for transfers between devices: 65.9 us -> 0 us
  matrix products: 27.3 us -> 0 us
  between operations: 14.5 us -> 0.64 us
  starting transfers between devices: 4.16 us -> 0 us
    all_gather x5 -> x0, blocking collectives: 152 us -> none  [compose(): lax.all_gather(right_vector, ('row', 'col'), axis=0, tiled=True)]
    pallas_call x0 -> x1, Pallas kernels: none -> 135 us  [shards(): pl.pallas_call(body, out_shape=(jax.ShapeDtypeStruct((nb, nb), BF), jax.S...]
    gather x10 -> x0, local copies, waits for them, and re-layouts: 112 us -> none  [the longest x5 65.4 us: compose(): moved = jnp.take(full_vector, pivots, axis=0)]
    ppermute x4 -> x0, waiting for transfers between devices: 34 us -> none  [from_behind(): lax.ppermute(value, axis, [(i, (i + by) % devices) for i in range(devices)])]
    all_gather x10 -> x0, waiting for transfers between devices: 29.3 us -> none  [the longest x5 28.9 us: compose(): segment = lax.all_gather(left_block, 'col', axis=1, tiled=True)]
    dot_general x10 -> x0, matrix products: 27.3 us -> none  [the longest x5 21.1 us: compose(): product = jnp.dot(segment, permuted, preferred_element_type=jnp.float32)]
    all_gather x3 -> x0, local copies, waits for them, and re-layouts: 8.63 us -> none  [compose(): column_panel = lax.all_gather(right_block, 'row', axis=0, tiled=True)]
  transfers between devices with their start and end apart: 14 -> 0, of which waited for: 9 -> 0; matrix products, arithmetic and copies ran while one was open for 31% -> 0% of each run, Pallas kernels for 0% -> 0%
where the time goes in v1:
time: 140 us
  Pallas kernels  135 us (96%)
  local copies, waits for them, and re-layouts  4.34 us (3%)
    pallas_call x1, Pallas kernels, shards(): pl.pallas_call(body, out_shape=(jax.ShapeDtypeStruct((nb, nb), BF), jax.S...  135 us
    unnamed x3, local copies, waits for them, and re-layouts  4.34 us

profile of v1, /device:TPU:1, one launch (start us, length us, event | category | flops | bytes accessed | tf_op | source)
XLA Modules:
  0.0 140.2 jit_solution(5100028547206003438)
XLA Ops:
  0.6 1.4 copy.8
  2.0 135.3 %newton.1 = (bf16[512,512]{1,0:T(8,128)(2,1)}, f32[1,128]{1,0:T(1,128)}) custom-call(bf16[4,512,512]{2,1,0:T(8,128)(2,1)} %bitcast.6, s32[3,2048]{1,0:T(4,128)} %bitcast.8, s32[16,2048]{1,0:T(8,128)} %bpiv_ref.1, bf16[4,128]{1,0:T(4,128)(2,1)} %bitcast.9), custom_call_target="tpu_custom_call" | custom-call | tf_op jit(solution)/shard_map/newton/pallas_call | solution.py:273
  137.3 1.9 %copy.11 = bf16[1,512,512]{2,1,0:T(8,128)(2,1)} copy(bf16[1,512,512]{2,1,0:T(8,128)(2,1)} %bitcast.7) | data formatting | bytes 1048576
  139.1 1.1 copy.12

commit v2 on v0

v2 whole, which is shorter than its diff:
```python
import jax
import jax.numpy as jnp
from jax import lax
from jax.experimental import pallas as pl
from jax.experimental.pallas import tpu as pltpu
from jax.sharding import PartitionSpec as P

MESH = pl.DeviceIdType.MESH
BF, F32 = jnp.bfloat16, jnp.float32
NT = (((1,), (1,)), ((), ()))

FIRST, SECOND, PASSED = 0, 1, 2
STAGES, HALVES, VECTOR = 5, 10, 4


def body(w_ref, ipiv_ref, bpiv_ref, res_ref, out_ref, rhs_ref, gath, panel, vecs, own_vec, relay, relay_vec, perm, hot, pivs,
         gsend, gbuf, rbuf, load_sem, gs_sem, gr_sem, ys_sem, yr_sem, ps_sem, pr_sem, rs_sem, rr_sem, fs_sem):
    loop, row, col = lax.axis_index("loop"), lax.axis_index("row"), lax.axis_index("col")
    n_loop, n_row, n_col = lax.axis_size("loop"), lax.axis_size("row"), lax.axis_size("col")
    nb = perm.shape[0]
    half, quarter = nb // 2, nb // 4
    share = res_ref.shape[1]
    odd = lax.rem(loop, 2) == 1
    even = lax.rem(loop, 2) == 0
    own_lanes = pl.ds(0, nb)

    def at(dloop=0, row_=None, dcol=0):
        return {
            "loop": lax.rem(loop + dloop + n_loop, n_loop),
            "row": row if row_ is None else row_,
            "col": lax.rem(col + dcol + n_col, n_col),
        }

    sibling = row + 1 - 2 * lax.rem(row, 2)
    across = lax.rem(row + 2, n_row)

    def copy(src, dst, ssem, rsem, dev):
        return pltpu.make_async_remote_copy(
            src_ref=src, dst_ref=dst, send_sem=ssem, recv_sem=rsem, device_id=dev, device_id_type=MESH
        )

    def y_copy(j, k, direction):
        s, h = lax.div(j, 2), lax.rem(j, 2)
        near = 1 + direction
        offset = (direction + (k == SECOND)) % 2 * quarter
        rows = pl.ds(pl.multiple_of(h * half + offset, quarter), quarter)
        near_lanes = pl.ds(near * nb, nb)
        if k == PASSED:
            src, dst = gath.at[s, rows, near_lanes], gath.at[s, rows, pl.ds(3 * nb, nb)]
        else:
            src, dst = gath.at[s, rows, own_lanes], gath.at[s, rows, near_lanes]
        return copy(src, dst, ys_sem.at[j, k, direction], yr_sem.at[j, k, direction], at(dcol=1 - 2 * direction))

    def y_issue(j, k):
        for direction in (0, 1):
            y_copy(j, k, direction).start()

    def y_recv(j, k):
        for direction in (0, 1):
            y_copy(j, k, direction).wait_recv()

    def part(t, slot, q):
        if q == VECTOR:
            return vecs.at[t, :, pl.ds(slot * nb, nb)]
        return panel.at[t, pl.ds(slot * nb + q * quarter, quarter)]

    def own_part(t, q):
        if q == VECTOR:
            return own_vec.at[t - 3]
        return gath.at[t, pl.ds(q * quarter, quarter), own_lanes]

    def p_copy(t, q, src, slot, dev):
        return copy(src, part(t, slot, q), ps_sem.at[t, slot, q], pr_sem.at[t, slot, q], dev)

    def local_sends(t, q):
        return [p_copy(t, q, part(t, 0, q), 1, at(row_=sibling)), p_copy(t, q, part(t, 0, q), 2, at(row_=across))]

    def next_sends(q):
        src = own_part(3, q)
        return [p_copy(3, q, src, 0, at(dloop=1)), p_copy(3, q, src, 2, at(dloop=1, row_=across))]

    def relay_part(q):
        return relay_vec if q == VECTOR else relay.at[pl.ds(q * quarter, quarter)]

    def relay_send(q):
        return copy(own_part(3, q), relay_part(q), rs_sem.at[q], rr_sem.at[q], at(dloop=2))

    def relay_passes(q):
        src = relay_part(q)
        return [p_copy(3, q, src, 0, at(dloop=-1)), p_copy(3, q, src, 2, at(dloop=-1, row_=across))]

    def far_send(q):
        return p_copy(4, q, own_part(4, q), 0, at(dloop=2))

    def to_sibling(t, q, slot):
        return copy(part(t, slot, q), part(t, slot + 1, q), fs_sem.at[t, slot // 2, q], pr_sem.at[t, slot + 1, q], at(row_=sibling))

    def p_recv(t, slot, q):
        p_copy(t, q, part(t, slot, q), slot, at(row_=sibling)).wait_recv()

    def far_forward(t, q):
        p_recv(t, 2, q)
        to_sibling(t, q, 2).start()

    def join(t):
        for q in range(5):
            p_recv(t, 1, q)
            p_recv(t, 3, q)

    def start_next(q):
        @pl.when(even)
        def _():
            for c in next_sends(q):
                c.start()

        @pl.when(odd)
        def _():
            relay_send(q).start()

    def pass_relay(qs):
        @pl.when(odd)
        def _():
            for q in qs:
                relay_send(q).wait_recv()
                for c in relay_passes(q):
                    c.start()

    def make_hot(s):
        for slot, dcol in enumerate((0, n_col - 1, 1, 2)):
            start = pl.multiple_of(lax.rem(col + dcol, n_col) * nb, nb)
            q = pivs[pl.ds(s, 1), pl.ds(start, nb)]

            def one(row_slot, carry):
                base = lax.rem(row + 2 * lax.div(row_slot, 2), n_row)
                base = base + (1 - 2 * lax.rem(base, 2)) * lax.rem(row_slot, 2)
                iota = lax.broadcasted_iota(jnp.int32, (nb, nb), 0)
                rows = pl.ds(pl.multiple_of(row_slot * nb, nb), nb)
                hot[rows, pl.ds(slot * nb, nb)] = jnp.where(iota == q - base * nb, 1.0, 0.0).astype(BF)
                return carry

            lax.fori_loop(0, 4, one, 0)

    def permute(j, lanes, first):
        s, h = lax.div(j, 2), lax.rem(j, 2)
        rows = pl.ds(pl.multiple_of(h * half, half), half)

        def one(part_, carry):
            targets = pl.ds(pl.multiple_of(part_ * 2 * nb, 2 * nb), 2 * nb)
            moved = lax.dot_general(gath[s, rows, lanes], hot[targets, lanes], NT, preferred_element_type=F32).astype(BF)
            if first:
                perm[rows, targets] = moved
            else:
                perm[rows, targets] += moved
            return carry

        lax.fori_loop(0, 2, one, 0)

    def product(s, h):
        rows = pl.ds(pl.multiple_of(h * half, half), half)
        value = jnp.dot(perm[rows, :], panel[s], preferred_element_type=F32).astype(BF)

        @pl.when(s < 2)
        def _():
            panel[s + 1, rows, :] = value

        @pl.when((s >= 2) & (s < 4))
        def _():
            gath[s + 1, rows, own_lanes] = value

        @pl.when(s == 4)
        def _():
            out_ref[rows, :] = value

    def finish_vector(s):
        rbuf[...] = lax.dot_general(vecs[s], perm[...], NT, preferred_element_type=F32)

        @pl.when(s < 3)
        def _():
            rbuf[...] += gbuf[pl.ds(s + 1, 1), :]

        @pl.when(s >= 3)
        def _():
            rbuf[...] += own_vec[s - 3].astype(F32)

        @pl.when(s < 2)
        def _():
            vecs[s + 1, :, own_lanes] = rbuf[...].astype(BF)

        @pl.when((s >= 2) & (s < 4))
        def _():
            own_vec[s - 2] = rbuf[...].astype(BF)

    loads = [pltpu.make_async_copy(w_ref.at[0], panel.at[0, pl.ds(0, nb)], load_sem.at[0])]
    for s in range(3):
        loads.append(pltpu.make_async_copy(w_ref.at[s + 1], gath.at[s, :, own_lanes], load_sem.at[s + 1]))
    for load in loads:
        load.start()
    barrier = pltpu.get_barrier_semaphore()
    partners = (
        at(dcol=1), at(dcol=-1), at(dcol=2), at(row_=sibling), at(row_=across),
        at(dloop=1), at(dloop=-1), at(dloop=1, row_=across), at(dloop=-1, row_=across), at(dloop=2), at(dloop=-2),
    )
    for partner in partners:
        pl.semaphore_signal(barrier, inc=1, device_id=partner, device_id_type=MESH)
    own_cols = pl.ds(pl.multiple_of(col * share, share), share)
    gsend[...] = jnp.zeros_like(gsend)
    gsend[pl.ds(0, 4), :] = res_ref[...].astype(F32)
    gbuf[:, own_cols] = gsend[...]
    pivs[pl.ds(0, 3), :] = ipiv_ref[...]
    pivs[pl.ds(3, 1), :] = bpiv_ref[pl.ds(loop, 1), :]
    pivs[pl.ds(4, 1), :] = bpiv_ref[pl.ds(lax.rem(loop + n_loop - 1, n_loop), 1), :]
    for load in loads:
        load.wait()
    pl.semaphore_wait(barrier, len(partners))

    def g_copy(i, dcol, holder):
        cols = pl.ds(pl.multiple_of(lax.rem(col + holder + n_col, n_col) * share, share), share)
        return copy(gsend, gbuf.at[:, cols], gs_sem.at[i], gr_sem.at[i], at(dcol=dcol))

    y_issue(0, FIRST)
    y_issue(0, SECOND)
    for i, dcol in enumerate((1, -1, 2)):
        g_copy(i, dcol, 0).start()
    for q in range(4):
        for c in local_sends(0, q):
            c.start()
    make_hot(0)
    for i, dcol in enumerate((-1, 1, 2)):
        g_copy(i, dcol, dcol).wait_recv()
    vecs[0, :, own_lanes] = jnp.broadcast_to(gbuf[pl.ds(0, 1), :], (16, nb)).astype(BF)
    for c in local_sends(0, VECTOR):
        c.start()

    def step(j, carry):
        s, h = lax.div(j, 2), lax.rem(j, 2)
        y_recv(j, FIRST)
        y_issue(j, PASSED)
        y_recv(j, SECOND)

        @pl.when(j < 5)
        def _():
            y_issue(j + 1, FIRST)
            y_issue(j + 1, SECOND)

        permute(j, pl.ds(0, 3 * nb), True)

        @pl.when((h == 1) & (s < 2))
        def _():
            for q in (0, 1):
                far_forward(s + 1, q)

        @pl.when(j == 0)
        def _():
            for q in (0, 1):
                far_forward(0, q)

        @pl.when((h == 0) & (s < 3))
        def _():
            for q in (2, 3, VECTOR):
                far_forward(s, q)

        @pl.when(j == 5)
        def _():
            pass_relay((0, 1))

        @pl.when(j == 6)
        def _():
            pass_relay((2, 3, VECTOR))
            for q in (0, 1):
                p_recv(3, 0, q)
                to_sibling(3, q, 0).start()
                far_forward(3, q)

        @pl.when(j == 7)
        def _():
            for q in (2, 3, VECTOR):
                p_recv(3, 0, q)
                to_sibling(3, q, 0).start()
                far_forward(3, q)
            join(3)

        def receive_far(q):
            p_recv(4, 0, q)
            for c in local_sends(4, q):
                c.start()

        @pl.when(j == 8)
        def _():
            for q in (0, 1):
                receive_far(q)

        @pl.when(j == 9)
        def _():
            for q in (2, 3, VECTOR):
                receive_far(q)
            for q in range(5):
                far_forward(4, q)
            join(4)

        @pl.when((h == 1) & (s >= 3))
        def _():
            product(s, 0)

        @pl.when(j == 7)
        def _():
            for q in (0, 1):
                far_send(q).start()
            y_issue(8, FIRST)
            y_issue(8, SECOND)

        y_recv(j, PASSED)
        permute(j, pl.ds(3 * nb, nb), False)

        @pl.when((h == 0) & (s < 3))
        def _():
            join(s)

        @pl.when((h == 1) | (s < 3))
        def _():
            product(s, h)

        @pl.when((j == 4) | (j == 5) | (j == 7))
        def _():
            y_issue(j + 2, FIRST)
            y_issue(j + 2, SECOND)

        for hh in (0, 1):
            @pl.when((h == hh) & (s < 2))
            def _():
                for q in (2 * hh, 2 * hh + 1):
                    for c in local_sends(s + 1, q):
                        c.start()

            @pl.when((h == hh) & (s == 2))
            def _():
                for q in (2 * hh, 2 * hh + 1):
                    start_next(q)

        @pl.when(j == 7)
        def _():
            for q in (2, 3):
                far_send(q).start()

        @pl.when(h == 1)
        def _():
            finish_vector(s)

        @pl.when((h == 1) & (s < 2))
        def _():
            for c in local_sends(s + 1, VECTOR):
                c.start()

        @pl.when(j == 5)
        def _():
            start_next(VECTOR)

        @pl.when(j == 7)
        def _():
            far_send(VECTOR).start()

        @pl.when((h == 1) & (s < 4))
        def _():
            make_hot(s + 1)

        return carry

    lax.fori_loop(0, HALVES, step, 0)
    rhs_ref[...] = rbuf[pl.ds(0, 1), own_cols]

    for i, dcol in enumerate((1, -1, 2)):
        g_copy(i, dcol, 0).wait_send()

    def drain(j, carry):
        for k in (FIRST, SECOND, PASSED):
            for direction in (0, 1):
                y_copy(j, k, direction).wait_send()
        return carry

    lax.fori_loop(0, HALVES, drain, 0)

    def drain_panel(t, carry):
        for q in range(5):
            for c in local_sends(t, q):
                c.wait_send()
            to_sibling(t, q, 2).wait_send()
        return carry

    lax.fori_loop(0, 3, drain_panel, 0)
    drain_panel(4, 0)
    for q in range(5):
        far_send(q).wait_send()
        to_sibling(3, q, 0).wait_send()
        to_sibling(3, q, 2).wait_send()
        for c in next_sends(q):
            c.wait_send()

    @pl.when(odd)
    def _():
        for q in range(5):
            relay_send(q).wait_send()


def shards(interval_blocks, interval_pivots, boundary_pivots, interval_residuals):
    blocks, pivots, residuals = interval_blocks[0], interval_pivots[0], interval_residuals[0]
    nb, share = blocks.shape[1], residuals.shape[1]
    vmem = pl.BlockSpec(memory_space=pltpu.VMEM)
    reduced, rhs = pl.pallas_call(
        body,
        out_shape=(jax.ShapeDtypeStruct((nb, nb), BF), jax.ShapeDtypeStruct((1, share), F32)),
        in_specs=[pl.BlockSpec(memory_space=pl.ANY)] + [vmem] * 3,
        out_specs=(vmem, vmem),
        scratch_shapes=[
            pltpu.VMEM((STAGES, nb, 4 * nb), BF),
            pltpu.VMEM((STAGES, 4 * nb, nb), BF),
            pltpu.VMEM((STAGES, 16, 4 * nb), BF),
            pltpu.VMEM((2, 16, nb), BF),
            pltpu.VMEM((nb, nb), BF),
            pltpu.VMEM((16, nb), BF),
            pltpu.VMEM((nb, 4 * nb), BF),
            pltpu.VMEM((4 * nb, 4 * nb), BF),
            pltpu.VMEM((8, 4 * nb), jnp.int32),
            pltpu.VMEM((8, share), F32),
            pltpu.VMEM((8, nb), F32),
            pltpu.VMEM((16, nb), F32),
            pltpu.SemaphoreType.DMA((4,)),
            pltpu.SemaphoreType.DMA((3,)),
            pltpu.SemaphoreType.DMA((3,)),
            pltpu.SemaphoreType.DMA((HALVES, 3, 2)),
            pltpu.SemaphoreType.DMA((HALVES, 3, 2)),
            pltpu.SemaphoreType.DMA((STAGES, 4, 5)),
            pltpu.SemaphoreType.DMA((STAGES, 4, 5)),
            pltpu.SemaphoreType.DMA((5,)),
            pltpu.SemaphoreType.DMA((5,)),
            pltpu.SemaphoreType.DMA((STAGES, 2, 5)),
        ],
        compiler_params=pltpu.CompilerParams(
            collective_id=0, has_side_effects=True, vmem_limit_bytes=60 * 2**20
        ),
        name="newton",
    )(blocks, pivots, boundary_pivots, residuals)
    return reduced[None], rhs


def solution(mesh):
    placed = (
        P("loop", None, "row", "col"),
        P("loop", None, None),
        P(),
        P("loop", None, ("row", "col")),
    )
    return jax.shard_map(
        shards,
        mesh=mesh,
        in_specs=placed,
        out_specs=(P("loop", "row", "col"), P("loop", ("row", "col"))),
        check_vma=False,
    )
```

time: 395 us -> 139 us (0.35)
  blocking collectives: 152 us -> 0 us
  Pallas kernels: 0 us -> 134 us
  local copies, waits for them, and re-layouts: 126 us -> 4.34 us
  waiting for transfers between devices: 65.9 us -> 0 us
  matrix products: 27.3 us -> 0 us
  between operations: 14.5 us -> 0.64 us
  starting transfers between devices: 4.16 us -> 0 us
    all_gather x5 -> x0, blocking collectives: 152 us -> none  [compose(): lax.all_gather(right_vector, ('row', 'col'), axis=0, tiled=True)]
    pallas_call x0 -> x1, Pallas kernels: none -> 134 us  [shards(): pl.pallas_call(body, out_shape=(jax.ShapeDtypeStruct((nb, nb), BF), jax.S...]
    gather x10 -> x0, local copies, waits for them, and re-layouts: 112 us -> none  [the longest x5 65.4 us: compose(): moved = jnp.take(full_vector, pivots, axis=0)]
    ppermute x4 -> x0, waiting for transfers between devices: 34 us -> none  [from_behind(): lax.ppermute(value, axis, [(i, (i + by) % devices) for i in range(devices)])]
    all_gather x10 -> x0, waiting for transfers between devices: 29.3 us -> none  [the longest x5 28.9 us: compose(): segment = lax.all_gather(left_block, 'col', axis=1, tiled=True)]
    dot_general x10 -> x0, matrix products: 27.3 us -> none  [the longest x5 21.1 us: compose(): product = jnp.dot(segment, permuted, preferred_element_type=jnp.float32)]
    all_gather x3 -> x0, local copies, waits for them, and re-layouts: 8.63 us -> none  [compose(): column_panel = lax.all_gather(right_block, 'row', axis=0, tiled=True)]
  transfers between devices with their start and end apart: 14 -> 0, of which waited for: 9 -> 0; matrix products, arithmetic and copies ran while one was open for 31% -> 0% of each run, Pallas kernels for 0% -> 0%
where the time goes in v2:
time: 139 us
  Pallas kernels  134 us (96%)
  local copies, waits for them, and re-layouts  4.34 us (3%)
    pallas_call x1, Pallas kernels, shards(): pl.pallas_call(body, out_shape=(jax.ShapeDtypeStruct((nb, nb), BF), jax.S...  134 us
    unnamed x3, local copies, waits for them, and re-layouts  4.34 us

profile of v2, /device:TPU:1, one launch (start us, length us, event | category | flops | bytes accessed | tf_op | source)
XLA Modules:
  0.0 138.7 jit_solution(8703072565843381709)
XLA Ops:
  0.6 1.4 copy.8
  2.0 133.7 %newton.1 = (bf16[512,512]{1,0:T(8,128)(2,1)}, f32[1,128]{1,0:T(1,128)}) custom-call(bf16[4,512,512]{2,1,0:T(8,128)(2,1)} %bitcast.6, s32[3,2048]{1,0:T(4,128)} %bitcast.8, s32[16,2048]{1,0:T(8,128)} %bpiv_ref.1, bf16[4,128]{1,0:T(4,128)(2,1)} %bitcast.9), custom_call_target="tpu_custom_call" | custom-call | tf_op jit(solution)/shard_map/newton/pallas_call | solution.py:407
  135.7 1.9 %copy.11 = bf16[1,512,512]{2,1,0:T(8,128)(2,1)} copy(bf16[1,512,512]{2,1,0:T(8,128)(2,1)} %bitcast.7) | data formatting | bytes 1048576
  137.6 1.1 copy.12

commit v3 on v2

--- a/solution.py
+++ b/solution.py
@@ -14,7 +14,7 @@
 
 
 def body(w_ref, ipiv_ref, bpiv_ref, res_ref, out_ref, rhs_ref, gath, panel, vecs, own_vec, relay, relay_vec, perm, hot, pivs,
-         gsend, gbuf, rbuf, load_sem, gs_sem, gr_sem, ys_sem, yr_sem, ps_sem, pr_sem, rs_sem, rr_sem, fs_sem):
+         gsend, gbuf, rbuf, held, load_sem, gs_sem, gr_sem, ys_sem, yr_sem, ps_sem, pr_sem, rs_sem, rr_sem, fs_sem):
     loop, row, col = lax.axis_index("loop"), lax.axis_index("row"), lax.axis_index("col")
     n_loop, n_row, n_col = lax.axis_size("loop"), lax.axis_size("row"), lax.axis_size("col")
     nb = perm.shape[0]
@@ -159,11 +159,11 @@
         rows = pl.ds(pl.multiple_of(h * half, half), half)
         value = jnp.dot(perm[rows, :], panel[s], preferred_element_type=F32).astype(BF)
 
-        @pl.when(s < 2)
-        def _():
-            panel[s + 1, rows, :] = value
-
-        @pl.when((s >= 2) & (s < 4))
+        @pl.when(s == 0)
+        def _():
+            panel[2, rows, :] = value
+
+        @pl.when((s >= 1) & (s < 4))
         def _():
             gath[s + 1, rows, own_lanes] = value
 
@@ -174,25 +174,34 @@
     def finish_vector(s):
         rbuf[...] = lax.dot_general(vecs[s], perm[...], NT, preferred_element_type=F32)
 
-        @pl.when(s < 3)
-        def _():
-            rbuf[...] += gbuf[pl.ds(s + 1, 1), :]
+        @pl.when(s < 2)
+        def _():
+            rbuf[...] += gbuf[pl.ds(2 * s + 1, 1), :]
+
+        @pl.when(s == 0)
+        def _():
+            vecs[2, :, own_lanes] = rbuf[...].astype(BF)
+
+        @pl.when(s == 1)
+        def _():
+            held[...] = rbuf[...]
+
+        @pl.when(s == 2)
+        def _():
+            rbuf[...] += held[...]
 
         @pl.when(s >= 3)
         def _():
             rbuf[...] += own_vec[s - 3].astype(F32)
 
-        @pl.when(s < 2)
-        def _():
-            vecs[s + 1, :, own_lanes] = rbuf[...].astype(BF)
-
         @pl.when((s >= 2) & (s < 4))
         def _():
             own_vec[s - 2] = rbuf[...].astype(BF)
 
-    loads = [pltpu.make_async_copy(w_ref.at[0], panel.at[0, pl.ds(0, nb)], load_sem.at[0])]
-    for s in range(3):
-        loads.append(pltpu.make_async_copy(w_ref.at[s + 1], gath.at[s, :, own_lanes], load_sem.at[s + 1]))
+    loads = []
+    for s in range(2):
+        loads.append(pltpu.make_async_copy(w_ref.at[2 * s + 1], gath.at[s, :, own_lanes], load_sem.at[2 * s]))
+        loads.append(pltpu.make_async_copy(w_ref.at[2 * s], panel.at[s, pl.ds(0, nb)], load_sem.at[2 * s + 1]))
     for load in loads:
         load.start()
     barrier = pltpu.get_barrier_semaphore()
@@ -206,7 +215,8 @@
     gsend[...] = jnp.zeros_like(gsend)
     gsend[pl.ds(0, 4), :] = res_ref[...].astype(F32)
     gbuf[:, own_cols] = gsend[...]
-    pivs[pl.ds(0, 3), :] = ipiv_ref[...]
+    for s, interval in enumerate((0, 2, 1)):
+        pivs[pl.ds(s, 1), :] = ipiv_ref[pl.ds(interval, 1), :]
     pivs[pl.ds(3, 1), :] = bpiv_ref[pl.ds(loop, 1), :]
     pivs[pl.ds(4, 1), :] = bpiv_ref[pl.ds(lax.rem(loop + n_loop - 1, n_loop), 1), :]
     for load in loads:
@@ -217,8 +227,9 @@
         cols = pl.ds(pl.multiple_of(lax.rem(col + holder + n_col, n_col) * share, share), share)
         return copy(gsend, gbuf.at[:, cols], gs_sem.at[i], gr_sem.at[i], at(dcol=dcol))
 
-    y_issue(0, FIRST)
-    y_issue(0, SECOND)
+    for j in (0, 1):
+        y_issue(j, FIRST)
+        y_issue(j, SECOND)
     for i, dcol in enumerate((1, -1, 2)):
         g_copy(i, dcol, 0).start()
     for q in range(4):
@@ -227,7 +238,8 @@
     make_hot(0)
     for i, dcol in enumerate((-1, 1, 2)):
         g_copy(i, dcol, dcol).wait_recv()
-    vecs[0, :, own_lanes] = jnp.broadcast_to(gbuf[pl.ds(0, 1), :], (16, nb)).astype(BF)
+    for s in (0, 1):
+        vecs[s, :, own_lanes] = jnp.broadcast_to(gbuf[pl.ds(2 * s, 1), :], (16, nb)).astype(BF)
     for c in local_sends(0, VECTOR):
         c.start()
 
@@ -237,27 +249,35 @@
         y_issue(j, PASSED)
         y_recv(j, SECOND)
 
-        @pl.when(j < 5)
-        def _():
-            y_issue(j + 1, FIRST)
-            y_issue(j + 1, SECOND)
+        for last, new in ((0, 2), (2, 3)):
+            @pl.when(j == last)
+            def _():
+                y_issue(new, FIRST)
+                y_issue(new, SECOND)
 
         permute(j, pl.ds(0, 3 * nb), True)
 
-        @pl.when((h == 1) & (s < 2))
+        @pl.when(j == 0)
+        def _():
+            for q in range(5):
+                far_forward(0, q)
+                for c in local_sends(1, q):
+                    c.start()
+
+        @pl.when(j == 1)
         def _():
             for q in (0, 1):
-                far_forward(s + 1, q)
-
-        @pl.when(j == 0)
-        def _():
-            for q in (0, 1):
-                far_forward(0, q)
-
-        @pl.when((h == 0) & (s < 3))
+                far_forward(1, q)
+
+        @pl.when(j == 2)
         def _():
             for q in (2, 3, VECTOR):
-                far_forward(s, q)
+                far_forward(1, q)
+
+        @pl.when(j == 3)
+        def _():
+            for q in range(5):
+                far_forward(2, q)
 
         @pl.when(j == 5)
         def _():
@@ -319,16 +339,16 @@
         def _():
             product(s, h)
 
-        @pl.when((j == 4) | (j == 5) | (j == 7))
+        @pl.when((j == 2) | (j == 3) | (j == 4) | (j == 5) | (j == 7))
         def _():
             y_issue(j + 2, FIRST)
             y_issue(j + 2, SECOND)
 
         for hh in (0, 1):
-            @pl.when((h == hh) & (s < 2))
+            @pl.when(j == hh)
             def _():
                 for q in (2 * hh, 2 * hh + 1):
-                    for c in local_sends(s + 1, q):
+                    for c in local_sends(2, q):
                         c.start()
 
             @pl.when((h == hh) & (s == 2))
@@ -345,9 +365,9 @@
         def _():
             finish_vector(s)
 
-        @pl.when((h == 1) & (s < 2))
-        def _():
-            for c in local_sends(s + 1, VECTOR):
+        @pl.when(j == 1)
+        def _():
+            for c in local_sends(2, VECTOR):
                 c.start()
 
         @pl.when(j == 5)
@@ -422,6 +442,7 @@
             pltpu.VMEM((8, share), F32),
             pltpu.VMEM((8, nb), F32),
             pltpu.VMEM((16, nb), F32),
+            pltpu.VMEM((16, nb), F32),
             pltpu.SemaphoreType.DMA((4,)),
             pltpu.SemaphoreType.DMA((3,)),
             pltpu.SemaphoreType.DMA((3,)),

time: 139 us -> 139 us (level)
  no operation moved by 1% of the time
where the time goes in v3:
time: 139 us
  Pallas kernels  134 us (96%)
  local copies, waits for them, and re-layouts  4.34 us (3%)
    pallas_call x1, Pallas kernels, shards(): pl.pallas_call(body, out_shape=(jax.ShapeDtypeStruct((nb, nb), BF), jax.S...  134 us
    unnamed x3, local copies, waits for them, and re-layouts  4.34 us

profile of v3, /device:TPU:1, one launch (start us, length us, event | category | flops | bytes accessed | tf_op | source)
XLA Modules:
  0.0 139.1 jit_solution(18296707589690165196)
XLA Ops:
  0.6 1.4 copy.8
  2.0 134.1 %newton.1 = (bf16[512,512]{1,0:T(8,128)(2,1)}, f32[1,128]{1,0:T(1,128)}) custom-call(bf16[4,512,512]{2,1,0:T(8,128)(2,1)} %bitcast.6, s32[3,2048]{1,0:T(4,128)} %bitcast.8, s32[16,2048]{1,0:T(8,128)} %bpiv_ref.1, bf16[4,128]{1,0:T(4,128)(2,1)} %bitcast.9), custom_call_target="tpu_custom_call" | custom-call | tf_op jit(solution)/shard_map/newton/pallas_call | solution.py:427
  136.1 1.9 %copy.11 = bf16[1,512,512]{2,1,0:T(8,128)(2,1)} copy(bf16[1,512,512]{2,1,0:T(8,128)(2,1)} %bitcast.7) | data formatting | bytes 1048576
  138.0 1.1 copy.12

commit v4 on v3

--- a/solution.py
+++ b/solution.py
@@ -117,13 +117,12 @@
         def _():
             relay_send(q).start()
 
-    def pass_relay(qs):
+    def pass_relay(q):
         @pl.when(odd)
         def _():
-            for q in qs:
-                relay_send(q).wait_recv()
-                for c in relay_passes(q):
-                    c.start()
+            relay_send(q).wait_recv()
+            for c in relay_passes(q):
+                c.start()
 
     def make_hot(s):
         for slot, dcol in enumerate((0, n_col - 1, 1, 2)):
@@ -245,143 +244,114 @@
 
     def step(j, carry):
         s, h = lax.div(j, 2), lax.rem(j, 2)
+
+        def on(number, *actions):
+            @pl.when(j == number)
+            def _():
+                for action, qs in actions:
+                    for q in qs:
+                        action(q)
+
+        def first_far(q):
+            far_forward(0, q)
+            for c in local_sends(1, q):
+                c.start()
+
+        def second_far(q):
+            far_forward(1, q)
+
+        def third_far(q):
+            far_forward(2, q)
+
+        def pass_next(q):
+            for slot in (0, 2):
+                p_recv(3, slot, q)
+                to_sibling(3, q, slot).start()
+
+        def receive_far(q):
+            p_recv(4, 0, q)
+            for c in local_sends(4, q):
+                c.start()
+
+        def last_far(q):
+            far_forward(4, q)
+
         y_recv(j, FIRST)
         y_issue(j, PASSED)
+        on(6, (pass_relay, (1,)), (pass_next, (0,)))
+        on(8, (receive_far, (0,)))
+
+        @pl.when((h == 0) & (s > 0))
+        def _():
+            make_hot(s)
+
+        on(8, (receive_far, (1,)))
         y_recv(j, SECOND)
-
         for last, new in ((0, 2), (2, 3)):
             @pl.when(j == last)
             def _():
                 y_issue(new, FIRST)
                 y_issue(new, SECOND)
 
+        on(6, (pass_next, (1,)), (pass_relay, (2,)))
+        on(7, (pass_next, (2,)))
+        on(9, (last_far, (1, 2)))
         permute(j, pl.ds(0, 3 * nb), True)
-
-        @pl.when(j == 0)
-        def _():
-            for q in range(5):
-                far_forward(0, q)
-                for c in local_sends(1, q):
-                    c.start()
-
-        @pl.when(j == 1)
-        def _():
-            for q in (0, 1):
-                far_forward(1, q)
-
-        @pl.when(j == 2)
-        def _():
-            for q in (2, 3, VECTOR):
-                far_forward(1, q)
-
-        @pl.when(j == 3)
-        def _():
-            for q in range(5):
-                far_forward(2, q)
-
-        @pl.when(j == 5)
-        def _():
-            pass_relay((0, 1))
-
-        @pl.when(j == 6)
-        def _():
-            pass_relay((2, 3, VECTOR))
-            for q in (0, 1):
-                p_recv(3, 0, q)
-                to_sibling(3, q, 0).start()
-                far_forward(3, q)
-
-        @pl.when(j == 7)
-        def _():
-            for q in (2, 3, VECTOR):
-                p_recv(3, 0, q)
-                to_sibling(3, q, 0).start()
-                far_forward(3, q)
-            join(3)
-
-        def receive_far(q):
-            p_recv(4, 0, q)
-            for c in local_sends(4, q):
-                c.start()
-
-        @pl.when(j == 8)
-        def _():
-            for q in (0, 1):
-                receive_far(q)
-
-        @pl.when(j == 9)
-        def _():
-            for q in (2, 3, VECTOR):
-                receive_far(q)
-            for q in range(5):
-                far_forward(4, q)
-            join(4)
-
-        @pl.when((h == 1) & (s >= 3))
-        def _():
-            product(s, 0)
-
-        @pl.when(j == 7)
-        def _():
-            for q in (0, 1):
-                far_send(q).start()
-            y_issue(8, FIRST)
-            y_issue(8, SECOND)
-
+        on(0, (first_far, (0, 1, 2, 3, VECTOR)))
+        on(1, (second_far, (0, 1)))
+        on(2, (second_far, (2, 3, VECTOR)))
+        on(3, (third_far, (0, 1, 2, 3, VECTOR)))
+        on(5, (pass_relay, (0,)))
+        on(6, (pass_relay, (3, VECTOR)))
+        on(7, (pass_next, (3, VECTOR)))
+        on(8, (receive_far, (2,)))
+        on(9, (last_far, (3, VECTOR)))
         y_recv(j, PASSED)
         permute(j, pl.ds(3 * nb, nb), False)
+        on(8, (receive_far, (3, VECTOR)), (last_far, (0,)))
 
         @pl.when((h == 0) & (s < 3))
         def _():
             join(s)
 
-        @pl.when((h == 1) | (s < 3))
-        def _():
-            product(s, h)
-
-        @pl.when((j == 2) | (j == 3) | (j == 4) | (j == 5) | (j == 7))
-        def _():
-            y_issue(j + 2, FIRST)
-            y_issue(j + 2, SECOND)
-
-        for hh in (0, 1):
-            @pl.when(j == hh)
+        on(7, (join, (3,)))
+        on(9, (join, (4,)))
+
+        def multiply(hh, carry):
+            product(s, hh)
+            return carry
+
+        low = jnp.where(s < 3, h, 0)
+        high = jnp.where((s < 3) | (h == 1), h + 1, 0)
+        lax.fori_loop(low, high, multiply, 0)
+
+        for done, new in ((2, (4,)), (3, (5,)), (4, (6,)), (5, (7,)), (7, (8, 9))):
+            @pl.when(j == done)
             def _():
-                for q in (2 * hh, 2 * hh + 1):
-                    for c in local_sends(2, q):
-                        c.start()
-
-            @pl.when((h == hh) & (s == 2))
-            def _():
-                for q in (2 * hh, 2 * hh + 1):
-                    start_next(q)
-
-        @pl.when(j == 7)
-        def _():
-            for q in (2, 3):
-                far_send(q).start()
+                for n in new:
+                    y_issue(n, FIRST)
+                    y_issue(n, SECOND)
+
+        def start_third(q):
+            for c in local_sends(2, q):
+                c.start()
+
+        def start_far(q):
+            far_send(q).start()
+
+        on(0, (start_third, (0, 1)))
+        on(1, (start_third, (2, 3)))
+        on(4, (start_next, (0, 1)))
+        on(5, (start_next, (2, 3)))
+        on(7, (start_far, (0, 1, 2, 3)))
 
         @pl.when(h == 1)
         def _():
             finish_vector(s)
 
-        @pl.when(j == 1)
-        def _():
-            for c in local_sends(2, VECTOR):
-                c.start()
-
-        @pl.when(j == 5)
-        def _():
-            start_next(VECTOR)
-
-        @pl.when(j == 7)
-        def _():
-            far_send(VECTOR).start()
-
-        @pl.when((h == 1) & (s < 4))
-        def _():
-            make_hot(s + 1)
-
+        on(1, (start_third, (VECTOR,)))
+        on(5, (start_next, (VECTOR,)))
+        on(7, (start_far, (VECTOR,)))
         return carry
 
     lax.fori_loop(0, HALVES, step, 0)

time: 139 us -> 135 us (0.971)
  Pallas kernels: 134 us -> 130 us
    pallas_call x1, Pallas kernels: 134 us -> 130 us  [shards(): pl.pallas_call(body, out_shape=(jax.ShapeDtypeStruct((nb, nb), BF), jax.S...]
where the time goes in v4:
time: 135 us
  Pallas kernels  130 us (96%)
  local copies, waits for them, and re-layouts  4.34 us (3%)
    pallas_call x1, Pallas kernels, shards(): pl.pallas_call(body, out_shape=(jax.ShapeDtypeStruct((nb, nb), BF), jax.S...  130 us
    unnamed x3, local copies, waits for them, and re-layouts  4.34 us

profile of v4, /device:TPU:1, one launch (start us, length us, event | category | flops | bytes accessed | tf_op | source)
XLA Modules:
  0.0 134.7 jit_solution(16761260004966424240)
XLA Ops:
  0.6 1.4 %copy.8 = s32[1,3,2048]{2,1,0:T(4,128)} copy(s32[1,3,2048]{2,0,1:T(1,128)} %param.5) | data formatting | bytes 49152
  2.0 129.7 %newton.1 = (bf16[512,512]{1,0:T(8,128)(2,1)}, f32[1,128]{1,0:T(1,128)}) custom-call(bf16[4,512,512]{2,1,0:T(8,128)(2,1)} %bitcast.6, s32[3,2048]{1,0:T(4,128)} %bitcast.8, s32[16,2048]{1,0:T(8,128)} %bpiv_ref.1, bf16[4,128]{1,0:T(4,128)(2,1)} %bitcast.9), custom_call_target="tpu_custom_call" | custom-call | tf_op jit(solution)/shard_map/newton/pallas_call | solution.py:397
  131.7 1.9 %copy.11 = bf16[1,512,512]{2,1,0:T(8,128)(2,1)} copy(bf16[1,512,512]{2,1,0:T(8,128)(2,1)} %bitcast.7) | data formatting | bytes 1048576
  133.6 1.1 copy.12

commit v5 on v4

--- a/solution.py
+++ b/solution.py
@@ -102,10 +102,13 @@
         p_recv(t, 2, q)
         to_sibling(t, q, 2).start()
 
+    def join_part(t, q):
+        p_recv(t, 1, q)
+        p_recv(t, 3, q)
+
     def join(t):
         for q in range(5):
-            p_recv(t, 1, q)
-            p_recv(t, 3, q)
+            join_part(t, q)
 
     def start_next(q):
         @pl.when(even)
@@ -242,6 +245,31 @@
     for c in local_sends(0, VECTOR):
         c.start()
 
+    def drain(j, carry):
+        for k in (FIRST, SECOND, PASSED):
+            for direction in (0, 1):
+                y_copy(j, k, direction).wait_send()
+        return carry
+
+    def drain_panel(t, carry):
+        for q in range(5):
+            for c in local_sends(t, q):
+                c.wait_send()
+            to_sibling(t, q, 2).wait_send()
+        return carry
+
+    def drain_next():
+        for q in range(5):
+            for slot in (0, 2):
+                to_sibling(3, q, slot).wait_send()
+            for c in next_sends(q):
+                c.wait_send()
+
+        @pl.when(odd)
+        def _():
+            for q in range(5):
+                relay_send(q).wait_send()
+
     def step(j, carry):
         s, h = lax.div(j, 2), lax.rem(j, 2)
 
@@ -276,8 +304,11 @@
         def last_far(q):
             far_forward(4, q)
 
-        y_recv(j, FIRST)
-        y_issue(j, PASSED)
+        @pl.when((j == 0) | (j == 6) | (j == 8))
+        def _():
+            y_recv(j, FIRST)
+            y_issue(j, PASSED)
+
         on(6, (pass_relay, (1,)), (pass_next, (0,)))
         on(8, (receive_far, (0,)))
 
@@ -287,7 +318,7 @@
 
         on(8, (receive_far, (1,)))
         y_recv(j, SECOND)
-        for last, new in ((0, 2), (2, 3)):
+        for last, new in ((0, 2), (1, 3)):
             @pl.when(j == last)
             def _():
                 y_issue(new, FIRST)
@@ -306,6 +337,11 @@
         on(7, (pass_next, (3, VECTOR)))
         on(8, (receive_far, (2,)))
         on(9, (last_far, (3, VECTOR)))
+        @pl.when((j < 5) | (j == 6) | (j == 8))
+        def _():
+            y_recv(j + 1, FIRST)
+            y_issue(j + 1, PASSED)
+
         y_recv(j, PASSED)
         permute(j, pl.ds(3 * nb, nb), False)
         on(8, (receive_far, (3, VECTOR)), (last_far, (0,)))
@@ -315,7 +351,16 @@
             join(s)
 
         on(7, (join, (3,)))
-        on(9, (join, (4,)))
+
+        @pl.when(j == 9)
+        def _():
+            join_part(4, VECTOR)
+            finish_vector(4)
+            lax.fori_loop(0, HALVES - 1, drain, 0)
+            lax.fori_loop(0, 3, drain_panel, 0)
+            drain_next()
+            for q in range(VECTOR):
+                join_part(4, q)
 
         def multiply(hh, carry):
             product(s, hh)
@@ -345,7 +390,7 @@
         on(5, (start_next, (2, 3)))
         on(7, (start_far, (0, 1, 2, 3)))
 
-        @pl.when(h == 1)
+        @pl.when((h == 1) & (s < 4))
         def _():
             finish_vector(s)
 
@@ -359,35 +404,10 @@
 
     for i, dcol in enumerate((1, -1, 2)):
         g_copy(i, dcol, 0).wait_send()
-
-    def drain(j, carry):
-        for k in (FIRST, SECOND, PASSED):
-            for direction in (0, 1):
-                y_copy(j, k, direction).wait_send()
-        return carry
-
-    lax.fori_loop(0, HALVES, drain, 0)
-
-    def drain_panel(t, carry):
-        for q in range(5):
-            for c in local_sends(t, q):
-                c.wait_send()
-            to_sibling(t, q, 2).wait_send()
-        return carry
-
-    lax.fori_loop(0, 3, drain_panel, 0)
+    drain(HALVES - 1, 0)
     drain_panel(4, 0)
     for q in range(5):
         far_send(q).wait_send()
-        to_sibling(3, q, 0).wait_send()
-        to_sibling(3, q, 2).wait_send()
-        for c in next_sends(q):
-            c.wait_send()
-
-    @pl.when(odd)
-    def _():
-        for q in range(5):
-            relay_send(q).wait_send()
 
 
 def shards(interval_blocks, interval_pivots, boundary_pivots, interval_residuals):

time: 135 us -> 126 us (0.933)
  Pallas kernels: 130 us -> 121 us
    pallas_call x1, Pallas kernels: 130 us -> 121 us  [shards(): pl.pallas_call(body, out_shape=(jax.ShapeDtypeStruct((nb, nb), BF), jax.S...]
where the time goes in v5:
time: 126 us
  Pallas kernels  121 us (96%)
  local copies, waits for them, and re-layouts  4.34 us (3%)
    pallas_call x1, Pallas kernels, shards(): pl.pallas_call(body, out_shape=(jax.ShapeDtypeStruct((nb, nb), BF), jax.S...  121 us
    unnamed x3, local copies, waits for them, and re-layouts  4.34 us

profile of v5, /device:TPU:1, one launch (start us, length us, event | category | flops | bytes accessed | tf_op | source)
XLA Modules:
  0.0 125.7 jit_solution(2553329644361140509)
XLA Ops:
  0.6 1.4 %copy.8 = s32[1,3,2048]{2,1,0:T(4,128)} copy(s32[1,3,2048]{2,0,1:T(1,128)} %param.5) | data formatting | bytes 49152
  2.0 120.7 %newton.1 = (bf16[512,512]{1,0:T(8,128)(2,1)}, f32[1,128]{1,0:T(1,128)}) custom-call(bf16[4,512,512]{2,1,0:T(8,128)(2,1)} %bitcast.6, s32[3,2048]{1,0:T(4,128)} %bitcast.8, s32[16,2048]{1,0:T(8,128)} %bpiv_ref.1, bf16[4,128]{1,0:T(4,128)(2,1)} %bitcast.9), custom_call_target="tpu_custom_call" | custom-call | tf_op jit(solution)/shard_map/newton/pallas_call | solution.py:417
  122.7 1.9 %copy.11 = bf16[1,512,512]{2,1,0:T(8,128)(2,1)} copy(bf16[1,512,512]{2,1,0:T(8,128)(2,1)} %bitcast.7) | data formatting | bytes 1048576
  124.5 1.1 copy.12

commit v6 on v5

--- a/solution.py
+++ b/solution.py
@@ -218,7 +218,7 @@
     gsend[pl.ds(0, 4), :] = res_ref[...].astype(F32)
     gbuf[:, own_cols] = gsend[...]
     for s, interval in enumerate((0, 2, 1)):
-        pivs[pl.ds(s, 1), :] = ipiv_ref[pl.ds(interval, 1), :]
+        pivs[pl.ds(s, 1), :] = ipiv_ref[0, pl.ds(interval, 1), :]
     pivs[pl.ds(3, 1), :] = bpiv_ref[pl.ds(loop, 1), :]
     pivs[pl.ds(4, 1), :] = bpiv_ref[pl.ds(lax.rem(loop + n_loop - 1, n_loop), 1), :]
     for load in loads:
@@ -312,10 +312,11 @@
         on(6, (pass_relay, (1,)), (pass_next, (0,)))
         on(8, (receive_far, (0,)))
 
-        @pl.when((h == 0) & (s > 0))
+        @pl.when((j == 2) | (j == 4) | (j == 6))
         def _():
             make_hot(s)
 
+        permute(j, own_lanes, True)
         on(8, (receive_far, (1,)))
         y_recv(j, SECOND)
         for last, new in ((0, 2), (1, 3)):
@@ -326,8 +327,15 @@
 
         on(6, (pass_next, (1,)), (pass_relay, (2,)))
         on(7, (pass_next, (2,)))
-        on(9, (last_far, (1, 2)))
-        permute(j, pl.ds(0, 3 * nb), True)
+        on(8, (receive_far, (2,)))
+        on(9, (last_far, (2,)))
+
+        @pl.when(j == 8)
+        def _():
+            y_recv(9, FIRST)
+            y_issue(9, PASSED)
+
+        permute(j, pl.ds(nb, 2 * nb), False)
         on(0, (first_far, (0, 1, 2, 3, VECTOR)))
         on(1, (second_far, (0, 1)))
         on(2, (second_far, (2, 3, VECTOR)))
@@ -335,20 +343,24 @@
         on(5, (pass_relay, (0,)))
         on(6, (pass_relay, (3, VECTOR)))
         on(7, (pass_next, (3, VECTOR)))
-        on(8, (receive_far, (2,)))
+        on(8, (receive_far, (3, VECTOR)), (last_far, (0,)))
         on(9, (last_far, (3, VECTOR)))
-        @pl.when((j < 5) | (j == 6) | (j == 8))
+        @pl.when((j < 5) | (j == 6))
         def _():
             y_recv(j + 1, FIRST)
             y_issue(j + 1, PASSED)
 
         y_recv(j, PASSED)
         permute(j, pl.ds(3 * nb, nb), False)
-        on(8, (receive_far, (3, VECTOR)), (last_far, (0,)))
+        on(8, (last_far, (1,)))
 
         @pl.when((h == 0) & (s < 3))
         def _():
             join(s)
+
+        @pl.when(j == 7)
+        def _():
+            make_hot(4)
 
         on(7, (join, (3,)))
 
@@ -411,7 +423,7 @@
 
 
 def shards(interval_blocks, interval_pivots, boundary_pivots, interval_residuals):
-    blocks, pivots, residuals = interval_blocks[0], interval_pivots[0], interval_residuals[0]
+    blocks, residuals = interval_blocks[0], interval_residuals[0]
     nb, share = blocks.shape[1], residuals.shape[1]
     vmem = pl.BlockSpec(memory_space=pltpu.VMEM)
     reduced, rhs = pl.pallas_call(
@@ -448,7 +460,7 @@
             collective_id=0, has_side_effects=True, vmem_limit_bytes=60 * 2**20
         ),
         name="newton",
-    )(blocks, pivots, boundary_pivots, residuals)
+    )(blocks, interval_pivots, boundary_pivots, residuals)
     return reduced[None], rhs
 
 

time: 126 us -> 126 us (level)
  no operation moved by 1% of the time
where the time goes in v6:
time: 126 us
  Pallas kernels  121 us (96%)
  local copies, waits for them, and re-layouts  4.34 us (3%)
    pallas_call x1, Pallas kernels, shards(): pl.pallas_call(body, out_shape=(jax.ShapeDtypeStruct((nb, nb), BF), jax.S...  121 us
    unnamed x3, local copies, waits for them, and re-layouts  4.34 us

profile of v6, /device:TPU:1, one launch (start us, length us, event | category | flops | bytes accessed | tf_op | source)
XLA Modules:
  0.0 125.6 jit_solution(13153433848465982052)
XLA Ops:
  0.6 1.4 %copy.6.ipiv_ref = s32[1,3,2048]{2,1,0:T(4,128)} copy(s32[1,3,2048]{2,0,1:T(1,128)} %param.5) | data formatting | bytes 49152 | tf_op args[1]
  2.0 120.6 %newton.1 = (bf16[512,512]{1,0:T(8,128)(2,1)}, f32[1,128]{1,0:T(1,128)}) custom-call(bf16[4,512,512]{2,1,0:T(8,128)(2,1)} %bitcast.3, s32[1,3,2048]{2,1,0:T(4,128)} %copy.6.ipiv_ref, s32[16,2048]{1,0:T(8,128)} %bpiv_ref.1, bf16[4,128]{1,0:T(4,128)(2,1)} %bitcast.5), custom_call_target="tpu_custom_call" | custom-call | tf_op jit(solution)/shard_map/newton/pallas_call | solution.py:429
  122.6 1.9 %copy.9 = bf16[1,512,512]{2,1,0:T(8,128)(2,1)} copy(bf16[1,512,512]{2,1,0:T(8,128)(2,1)} %bitcast.4) | data formatting | bytes 1048576
  124.5 1.1 copy.10

commit v7 on v6

--- a/solution.py
+++ b/solution.py
@@ -135,9 +135,10 @@
             def one(row_slot, carry):
                 base = lax.rem(row + 2 * lax.div(row_slot, 2), n_row)
                 base = base + (1 - 2 * lax.rem(base, 2)) * lax.rem(row_slot, 2)
-                iota = lax.broadcasted_iota(jnp.int32, (nb, nb), 0)
+                iota = lax.broadcasted_iota(jnp.int16, (nb, nb), 0)
+                wanted = jnp.broadcast_to((q - base * nb).astype(jnp.int16), (nb, nb))
                 rows = pl.ds(pl.multiple_of(row_slot * nb, nb), nb)
-                hot[rows, pl.ds(slot * nb, nb)] = jnp.where(iota == q - base * nb, 1.0, 0.0).astype(BF)
+                hot[rows, pl.ds(slot * nb, nb)] = jnp.where(iota == wanted, BF(1), BF(0))
                 return carry
 
             lax.fori_loop(0, 4, one, 0)
@@ -218,7 +219,7 @@
     gsend[pl.ds(0, 4), :] = res_ref[...].astype(F32)
     gbuf[:, own_cols] = gsend[...]
     for s, interval in enumerate((0, 2, 1)):
-        pivs[pl.ds(s, 1), :] = ipiv_ref[0, pl.ds(interval, 1), :]
+        pivs[pl.ds(s, 1), :] = ipiv_ref[interval]
     pivs[pl.ds(3, 1), :] = bpiv_ref[pl.ds(loop, 1), :]
     pivs[pl.ds(4, 1), :] = bpiv_ref[pl.ds(lax.rem(loop + n_loop - 1, n_loop), 1), :]
     for load in loads:
@@ -358,9 +359,6 @@
         def _():
             join(s)
 
-        @pl.when(j == 7)
-        def _():
-            make_hot(4)
 
         on(7, (join, (3,)))
 
@@ -408,7 +406,7 @@
 
         on(1, (start_third, (VECTOR,)))
         on(5, (start_next, (VECTOR,)))
-        on(7, (start_far, (VECTOR,)))
+        on(7, (start_far, (VECTOR,)), (make_hot, (4,)))
         return carry
 
     lax.fori_loop(0, HALVES, step, 0)
@@ -460,7 +458,7 @@
             collective_id=0, has_side_effects=True, vmem_limit_bytes=60 * 2**20
         ),
         name="newton",
-    )(blocks, interval_pivots, boundary_pivots, residuals)
+    )(blocks, jnp.transpose(interval_pivots, (1, 0, 2)), boundary_pivots, residuals)
     return reduced[None], rhs
 
 

time: 126 us -> 123 us (0.976)
  Pallas kernels: 121 us -> 119 us
  local copies, waits for them, and re-layouts: 4.34 us -> 2.97 us
    unnamed x3 -> x2, local copies, waits for them, and re-layouts: 4.34 us -> 2.97 us
    pallas_call x1, Pallas kernels: 121 us -> 119 us  [shards(): pl.pallas_call(body, out_shape=(jax.ShapeDtypeStruct((nb, nb), BF), jax.S...]
where the time goes in v7:
time: 123 us
  Pallas kernels  119 us (97%)
  local copies, waits for them, and re-layouts  2.97 us (2%)
    pallas_call x1, Pallas kernels, shards(): pl.pallas_call(body, out_shape=(jax.ShapeDtypeStruct((nb, nb), BF), jax.S...  119 us
    unnamed x2, local copies, waits for them, and re-layouts  2.97 us

profile of v7, /device:TPU:1, one launch (start us, length us, event | category | flops | bytes accessed | tf_op | source)
XLA Modules:
  0.0 123.0 jit_solution(712321035035142426)
XLA Ops:
  0.6 119.3 %newton.1 = (bf16[512,512]{1,0:T(8,128)(2,1)}, f32[1,128]{1,0:T(1,128)}) custom-call(bf16[4,512,512]{2,1,0:T(8,128)(2,1)} %bitcast.4, s32[3,1,2048]{2,1,0:T(1,128)} %bitcast.6, s32[16,2048]{1,0:T(8,128)} %bpiv_ref.1, bf16[4,128]{1,0:T(4,128)(2,1)} %bitcast.7), custom_call_target="tpu_custom_call" | custom-call | tf_op jit(solution)/shard_map/newton/pallas_call | solution.py:427
  120.0 1.9 %copy.8 = bf16[1,512,512]{2,1,0:T(8,128)(2,1)} copy(bf16[1,512,512]{2,1,0:T(8,128)(2,1)} %bitcast.5) | data formatting | bytes 1048576
  121.8 1.1 copy.9

commit v8 on v7

--- a/solution.py
+++ b/solution.py
@@ -11,9 +11,10 @@
 
 FIRST, SECOND, PASSED = 0, 1, 2
 STAGES, HALVES, VECTOR = 5, 10, 4
-
-
-def body(w_ref, ipiv_ref, bpiv_ref, res_ref, out_ref, rhs_ref, gath, panel, vecs, own_vec, relay, relay_vec, perm, hot, pivs,
+RELAYED = (0, 2)
+
+
+def body(w_ref, ipiv_ref, bpiv_ref, res_ref, out_ref, rhs_ref, gath, panel, vecs, own_vec, relay, perm, hot, pivs,
          gsend, gbuf, rbuf, held, load_sem, gs_sem, gr_sem, ys_sem, yr_sem, ps_sem, pr_sem, rs_sem, rr_sem, fs_sem):
     loop, row, col = lax.axis_index("loop"), lax.axis_index("row"), lax.axis_index("col")
     n_loop, n_row, n_col = lax.axis_size("loop"), lax.axis_size("row"), lax.axis_size("col")
@@ -80,7 +81,7 @@
         return [p_copy(3, q, src, 0, at(dloop=1)), p_copy(3, q, src, 2, at(dloop=1, row_=across))]
 
     def relay_part(q):
-        return relay_vec if q == VECTOR else relay.at[pl.ds(q * quarter, quarter)]
+        return relay.at[pl.ds(q * quarter, quarter)]
 
     def relay_send(q):
         return copy(own_part(3, q), relay_part(q), rs_sem.at[q], rr_sem.at[q], at(dloop=2))
@@ -111,6 +112,11 @@
             join_part(t, q)
 
     def start_next(q):
+        if q not in RELAYED:
+            for c in next_sends(q):
+                c.start()
+            return
+
         @pl.when(even)
         def _():
             for c in next_sends(q):
@@ -268,7 +274,7 @@
 
         @pl.when(odd)
         def _():
-            for q in range(5):
+            for q in RELAYED:
                 relay_send(q).wait_send()
 
     def step(j, carry):
@@ -310,7 +316,7 @@
             y_recv(j, FIRST)
             y_issue(j, PASSED)
 
-        on(6, (pass_relay, (1,)), (pass_next, (0,)))
+        on(6, (pass_next, (0,)))
         on(8, (receive_far, (0,)))
 
         @pl.when((j == 2) | (j == 4) | (j == 6))
@@ -342,7 +348,6 @@
         on(2, (second_far, (2, 3, VECTOR)))
         on(3, (third_far, (0, 1, 2, 3, VECTOR)))
         on(5, (pass_relay, (0,)))
-        on(6, (pass_relay, (3, VECTOR)))
         on(7, (pass_next, (3, VECTOR)))
         on(8, (receive_far, (3, VECTOR)), (last_far, (0,)))
         on(9, (last_far, (3, VECTOR)))
@@ -418,6 +423,17 @@
     drain_panel(4, 0)
     for q in range(5):
         far_send(q).wait_send()
+
+
+def deliver(block_ref, rhs_ref, block_out, rhs_out, sems):
+    copies = [
+        pltpu.make_async_copy(block_ref, block_out, sems.at[0]),
+        pltpu.make_async_copy(rhs_ref, rhs_out, sems.at[1]),
+    ]
+    for copy in copies:
+        copy.start()
+    for copy in copies:
+        copy.wait()
 
 
 def shards(interval_blocks, interval_pivots, boundary_pivots, interval_residuals):
@@ -435,7 +451,6 @@
             pltpu.VMEM((STAGES, 16, 4 * nb), BF),
             pltpu.VMEM((2, 16, nb), BF),
             pltpu.VMEM((nb, nb), BF),
-            pltpu.VMEM((16, nb), BF),
             pltpu.VMEM((nb, 4 * nb), BF),
             pltpu.VMEM((4 * nb, 4 * nb), BF),
             pltpu.VMEM((8, 4 * nb), jnp.int32),
@@ -459,6 +474,15 @@
         ),
         name="newton",
     )(blocks, jnp.transpose(interval_pivots, (1, 0, 2)), boundary_pivots, residuals)
+    anywhere = pl.BlockSpec(memory_space=pl.ANY)
+    reduced, rhs = pl.pallas_call(
+        deliver,
+        out_shape=(jax.ShapeDtypeStruct((nb, nb), BF), jax.ShapeDtypeStruct((1, share), F32)),
+        in_specs=[anywhere] * 2,
+        out_specs=(anywhere, anywhere),
+        scratch_shapes=[pltpu.SemaphoreType.DMA((2,))],
+        name="deliver",
+    )(reduced, rhs)
     return reduced[None], rhs
 
 

time: 123 us -> 137 us (1.11)
  Pallas kernels: 119 us -> 136 us
  local copies, waits for them, and re-layouts: 2.97 us -> 0 us
    pallas_call x0 -> x1, Pallas kernels: none -> 17 us  [shards(): pl.pallas_call(deliver, out_shape=(jax.ShapeDtypeStruct((nb, nb), BF), ja...]
    unnamed x2 -> x0, local copies, waits for them, and re-layouts: 2.97 us -> none
where the time goes in v8:
time: 137 us
  Pallas kernels  136 us (99%)
    pallas_call x1, Pallas kernels, shards(): pl.pallas_call(body, out_shape=(jax.ShapeDtypeStruct((nb, nb), BF), jax.S...  119 us
    pallas_call x1, Pallas kernels, shards(): pl.pallas_call(deliver, out_shape=(jax.ShapeDtypeStruct((nb, nb), BF), ja...  17 us

profile of v8, /device:TPU:1, one launch (start us, length us, event | category | flops | bytes accessed | tf_op | source)
XLA Modules:
  0.0 136.9 jit_solution(1337162981278453880)
XLA Ops:
  0.6 119.3 %newton.1 = (bf16[512,512]{1,0:T(8,128)(2,1)}, f32[1,128]{1,0:T(1,128)}) custom-call(bf16[4,512,512]{2,1,0:T(8,128)(2,1)} %bitcast.4, s32[3,1,2048]{2,1,0:T(1,128)} %bitcast.5, s32[16,2048]{1,0:T(8,128)} %bpiv_ref.1, bf16[4,128]{1,0:T(4,128)(2,1)} %bitcast.6), custom_call_target="tpu_custom_call" | custom-call | tf_op jit(solution)/shard_map/newton/pallas_call | solution.py:443
  119.9 17.0 %deliver.1 = (bf16[512,512]{1,0:T(8,128)(2,1)}, f32[1,128]{1,0:T(1,128)}) custom-call(bf16[512,512]{1,0:T(8,128)(2,1)} %get-tuple-element.6.block_ref, f32[1,128]{1,0:T(1,128)} %get-tuple-element.7.rhs_ref), custom_call_target="tpu_custom_call" | custom-call | tf_op jit(solution)/shard_map/deliver/pallas_call | solution.py:478

commit v9 on v8

--- a/solution.py
+++ b/solution.py
@@ -11,10 +11,9 @@
 
 FIRST, SECOND, PASSED = 0, 1, 2
 STAGES, HALVES, VECTOR = 5, 10, 4
-RELAYED = (0, 2)
-
-
-def body(w_ref, ipiv_ref, bpiv_ref, res_ref, out_ref, rhs_ref, gath, panel, vecs, own_vec, relay, perm, hot, pivs,
+
+
+def body(w_ref, ipiv_hbm, bpiv_hbm, res_hbm, out_ref, rhs_ref, ipiv_ref, bpiv_ref, res_ref, gath, panel, vecs, own_vec, relay, relay_vec, perm, hot, pivs,
          gsend, gbuf, rbuf, held, load_sem, gs_sem, gr_sem, ys_sem, yr_sem, ps_sem, pr_sem, rs_sem, rr_sem, fs_sem):
     loop, row, col = lax.axis_index("loop"), lax.axis_index("row"), lax.axis_index("col")
     n_loop, n_row, n_col = lax.axis_size("loop"), lax.axis_size("row"), lax.axis_size("col")
@@ -81,7 +80,7 @@
         return [p_copy(3, q, src, 0, at(dloop=1)), p_copy(3, q, src, 2, at(dloop=1, row_=across))]
 
     def relay_part(q):
-        return relay.at[pl.ds(q * quarter, quarter)]
+        return relay_vec if q == VECTOR else relay.at[pl.ds(q * quarter, quarter)]
 
     def relay_send(q):
         return copy(own_part(3, q), relay_part(q), rs_sem.at[q], rr_sem.at[q], at(dloop=2))
@@ -112,11 +111,6 @@
             join_part(t, q)
 
     def start_next(q):
-        if q not in RELAYED:
-            for c in next_sends(q):
-                c.start()
-            return
-
         @pl.when(even)
         def _():
             for c in next_sends(q):
@@ -211,7 +205,11 @@
     for s in range(2):
         loads.append(pltpu.make_async_copy(w_ref.at[2 * s + 1], gath.at[s, :, own_lanes], load_sem.at[2 * s]))
         loads.append(pltpu.make_async_copy(w_ref.at[2 * s], panel.at[s, pl.ds(0, nb)], load_sem.at[2 * s + 1]))
-    for load in loads:
+    small = [
+        pltpu.make_async_copy(src, dst, load_sem.at[4 + i])
+        for i, (src, dst) in enumerate(((ipiv_hbm, ipiv_ref), (bpiv_hbm, bpiv_ref), (res_hbm, res_ref)))
+    ]
+    for load in small + loads:
         load.start()
     barrier = pltpu.get_barrier_semaphore()
     partners = (
@@ -221,6 +219,8 @@
     for partner in partners:
         pl.semaphore_signal(barrier, inc=1, device_id=partner, device_id_type=MESH)
     own_cols = pl.ds(pl.multiple_of(col * share, share), share)
+    for load in small:
+        load.wait()
     gsend[...] = jnp.zeros_like(gsend)
     gsend[pl.ds(0, 4), :] = res_ref[...].astype(F32)
     gbuf[:, own_cols] = gsend[...]
@@ -274,7 +274,7 @@
 
         @pl.when(odd)
         def _():
-            for q in RELAYED:
+            for q in range(5):
                 relay_send(q).wait_send()
 
     def step(j, carry):
@@ -316,7 +316,7 @@
             y_recv(j, FIRST)
             y_issue(j, PASSED)
 
-        on(6, (pass_next, (0,)))
+        on(6, (pass_relay, (1,)), (pass_next, (0,)))
         on(8, (receive_far, (0,)))
 
         @pl.when((j == 2) | (j == 4) | (j == 6))
@@ -348,6 +348,7 @@
         on(2, (second_far, (2, 3, VECTOR)))
         on(3, (third_far, (0, 1, 2, 3, VECTOR)))
         on(5, (pass_relay, (0,)))
+        on(6, (pass_relay, (3, VECTOR)))
         on(7, (pass_next, (3, VECTOR)))
         on(8, (receive_far, (3, VECTOR)), (last_far, (0,)))
         on(9, (last_far, (3, VECTOR)))
@@ -440,17 +441,23 @@
     blocks, residuals = interval_blocks[0], interval_residuals[0]
     nb, share = blocks.shape[1], residuals.shape[1]
     vmem = pl.BlockSpec(memory_space=pltpu.VMEM)
+    anywhere = pl.BlockSpec(memory_space=pl.ANY)
+    interval_rows = jnp.transpose(interval_pivots, (1, 0, 2))
     reduced, rhs = pl.pallas_call(
         body,
         out_shape=(jax.ShapeDtypeStruct((nb, nb), BF), jax.ShapeDtypeStruct((1, share), F32)),
-        in_specs=[pl.BlockSpec(memory_space=pl.ANY)] + [vmem] * 3,
+        in_specs=[anywhere] * 4,
         out_specs=(vmem, vmem),
         scratch_shapes=[
+            pltpu.VMEM(interval_rows.shape, jnp.int32),
+            pltpu.VMEM(boundary_pivots.shape, jnp.int32),
+            pltpu.VMEM(residuals.shape, BF),
             pltpu.VMEM((STAGES, nb, 4 * nb), BF),
             pltpu.VMEM((STAGES, 4 * nb, nb), BF),
             pltpu.VMEM((STAGES, 16, 4 * nb), BF),
             pltpu.VMEM((2, 16, nb), BF),
             pltpu.VMEM((nb, nb), BF),
+            pltpu.VMEM((16, nb), BF),
             pltpu.VMEM((nb, 4 * nb), BF),
             pltpu.VMEM((4 * nb, 4 * nb), BF),
             pltpu.VMEM((8, 4 * nb), jnp.int32),
@@ -458,7 +465,7 @@
             pltpu.VMEM((8, nb), F32),
             pltpu.VMEM((16, nb), F32),
             pltpu.VMEM((16, nb), F32),
-            pltpu.SemaphoreType.DMA((4,)),
+            pltpu.SemaphoreType.DMA((7,)),
             pltpu.SemaphoreType.DMA((3,)),
             pltpu.SemaphoreType.DMA((3,)),
             pltpu.SemaphoreType.DMA((HALVES, 3, 2)),
@@ -473,13 +480,12 @@
             collective_id=0, has_side_effects=True, vmem_limit_bytes=60 * 2**20
         ),
         name="newton",
-    )(blocks, jnp.transpose(interval_pivots, (1, 0, 2)), boundary_pivots, residuals)
-    anywhere = pl.BlockSpec(memory_space=pl.ANY)
+    )(blocks, interval_rows, boundary_pivots, residuals)
     reduced, rhs = pl.pallas_call(
         deliver,
         out_shape=(jax.ShapeDtypeStruct((nb, nb), BF), jax.ShapeDtypeStruct((1, share), F32)),
         in_specs=[anywhere] * 2,
-        out_specs=(anywhere, anywhere),
+        out_specs=(vmem, vmem),
         scratch_shapes=[pltpu.SemaphoreType.DMA((2,))],
         name="deliver",
     )(reduced, rhs)

time: 137 us -> 121 us (0.88)
  Pallas kernels: 136 us -> 120 us
    pallas_call x1, Pallas kernels: 17 us -> 1.86 us  [shards(): pl.pallas_call(deliver, out_shape=(jax.ShapeDtypeStruct((nb, nb), BF), ja...]
where the time goes in v9:
time: 121 us
  Pallas kernels  120 us (99%)
    pallas_call x1, Pallas kernels, shards(): pl.pallas_call(body, out_shape=(jax.ShapeDtypeStruct((nb, nb), BF), jax.S...  119 us

profile of v9, /device:TPU:1, one launch (start us, length us, event | category | flops | bytes accessed | tf_op | source)
XLA Modules:
  0.0 121.1 jit_solution(6292192111299818154)
XLA Ops:
  0.6 118.6 %newton.1 = (bf16[512,512]{1,0:T(8,128)(2,1)}, f32[1,128]{1,0:T(1,128)}) custom-call(bf16[4,512,512]{2,1,0:T(8,128)(2,1)} %bitcast.4, s32[3,1,2048]{2,1,0:T(1,128)} %bitcast.5, s32[16,2048]{1,0:T(8,128)} %bpiv_hbm.1, bf16[4,128]{1,0:T(4,128)(2,1)} %bitcast.6), custom_call_target="tpu_custom_call" | custom-call | tf_op jit(solution)/shard_map/newton/pallas_call | solution.py:446
  119.2 1.9 %deliver.1 = (bf16[512,512]{1,0:T(8,128)(2,1)}, f32[1,128]{1,0:T(1,128)}) custom-call(bf16[512,512]{1,0:T(8,128)(2,1)} %get-tuple-element.6.block_ref, f32[1,128]{1,0:T(1,128)} %get-tuple-element.7.rhs_ref), custom_call_target="tpu_custom_call" | custom-call | tf_op jit(solution)/shard_map/deliver/pallas_call | solution.py:484

commit v10 on v9

--- a/solution.py
+++ b/solution.py
@@ -138,7 +138,7 @@
                 iota = lax.broadcasted_iota(jnp.int16, (nb, nb), 0)
                 wanted = jnp.broadcast_to((q - base * nb).astype(jnp.int16), (nb, nb))
                 rows = pl.ds(pl.multiple_of(row_slot * nb, nb), nb)
-                hot[rows, pl.ds(slot * nb, nb)] = jnp.where(iota == wanted, BF(1), BF(0))
+                hot[lax.rem(s, 2), rows, pl.ds(slot * nb, nb)] = jnp.where(iota == wanted, BF(1), BF(0))
                 return carry
 
             lax.fori_loop(0, 4, one, 0)
@@ -149,7 +149,7 @@
 
         def one(part_, carry):
             targets = pl.ds(pl.multiple_of(part_ * 2 * nb, 2 * nb), 2 * nb)
-            moved = lax.dot_general(gath[s, rows, lanes], hot[targets, lanes], NT, preferred_element_type=F32).astype(BF)
+            moved = lax.dot_general(gath[s, rows, lanes], hot[lax.rem(s, 2), targets, lanes], NT, preferred_element_type=F32).astype(BF)
             if first:
                 perm[rows, targets] = moved
             else:
@@ -319,10 +319,6 @@
         on(6, (pass_relay, (1,)), (pass_next, (0,)))
         on(8, (receive_far, (0,)))
 
-        @pl.when((j == 2) | (j == 4) | (j == 6))
-        def _():
-            make_hot(s)
-
         permute(j, own_lanes, True)
         on(8, (receive_far, (1,)))
         y_recv(j, SECOND)
@@ -386,6 +382,14 @@
         high = jnp.where((s < 3) | (h == 1), h + 1, 0)
         lax.fori_loop(low, high, multiply, 0)
 
+        def start_third(q):
+            for c in local_sends(2, q):
+                c.start()
+
+        def start_far(q):
+            far_send(q).start()
+
+        on(5, (start_next, (2, 3)))
         for done, new in ((2, (4,)), (3, (5,)), (4, (6,)), (5, (7,)), (7, (8, 9))):
             @pl.when(j == done)
             def _():
@@ -393,17 +397,9 @@
                     y_issue(n, FIRST)
                     y_issue(n, SECOND)
 
-        def start_third(q):
-            for c in local_sends(2, q):
-                c.start()
-
-        def start_far(q):
-            far_send(q).start()
-
         on(0, (start_third, (0, 1)))
         on(1, (start_third, (2, 3)))
         on(4, (start_next, (0, 1)))
-        on(5, (start_next, (2, 3)))
         on(7, (start_far, (0, 1, 2, 3)))
 
         @pl.when((h == 1) & (s < 4))
@@ -412,7 +408,12 @@
 
         on(1, (start_third, (VECTOR,)))
         on(5, (start_next, (VECTOR,)))
-        on(7, (start_far, (VECTOR,)), (make_hot, (4,)))
+        on(7, (start_far, (VECTOR,)))
+
+        @pl.when((h == 0) & (s < 4))
+        def _():
+            make_hot(s + 1)
+
         return carry
 
     lax.fori_loop(0, HALVES, step, 0)
@@ -459,7 +460,7 @@
             pltpu.VMEM((nb, nb), BF),
             pltpu.VMEM((16, nb), BF),
             pltpu.VMEM((nb, 4 * nb), BF),
-            pltpu.VMEM((4 * nb, 4 * nb), BF),
+            pltpu.VMEM((2, 4 * nb, 4 * nb), BF),
             pltpu.VMEM((8, 4 * nb), jnp.int32),
             pltpu.VMEM((8, share), F32),
             pltpu.VMEM((8, nb), F32),

time: 121 us -> 121 us (level)
  no operation moved by 1% of the time
where the time goes in v10:
time: 121 us
  Pallas kernels  120 us (99%)
    pallas_call x1, Pallas kernels, shards(): pl.pallas_call(body, out_shape=(jax.ShapeDtypeStruct((nb, nb), BF), jax.S...  118 us

profile of v10, /device:TPU:1, one launch (start us, length us, event | category | flops | bytes accessed | tf_op | source)
XLA Modules:
  0.0 120.9 jit_solution(9891454034417150698)
XLA Ops:
  0.6 118.4 %newton.1 = (bf16[512,512]{1,0:T(8,128)(2,1)}, f32[1,128]{1,0:T(1,128)}) custom-call(bf16[4,512,512]{2,1,0:T(8,128)(2,1)} %bitcast.4, s32[3,1,2048]{2,1,0:T(1,128)} %bitcast.5, s32[16,2048]{1,0:T(8,128)} %bpiv_hbm.1, bf16[4,128]{1,0:T(4,128)(2,1)} %bitcast.6), custom_call_target="tpu_custom_call" | custom-call | tf_op jit(solution)/shard_map/newton/pallas_call | solution.py:447
  119.0 1.9 %deliver.1 = (bf16[512,512]{1,0:T(8,128)(2,1)}, f32[1,128]{1,0:T(1,128)}) custom-call(bf16[512,512]{1,0:T(8,128)(2,1)} %get-tuple-element.6.block_ref, f32[1,128]{1,0:T(1,128)} %get-tuple-element.7.rhs_ref), custom_call_target="tpu_custom_call" | custom-call | tf_op jit(solution)/shard_map/deliver/pallas_call | solution.py:485

commit v11 on v10

--- a/solution.py
+++ b/solution.py
@@ -317,6 +317,12 @@
             y_issue(j, PASSED)
 
         on(6, (pass_relay, (1,)), (pass_next, (0,)))
+
+        @pl.when(j == 8)
+        def _():
+            y_recv(9, FIRST)
+            y_issue(9, PASSED)
+
         on(8, (receive_far, (0,)))
 
         permute(j, own_lanes, True)
@@ -332,11 +338,6 @@
         on(7, (pass_next, (2,)))
         on(8, (receive_far, (2,)))
         on(9, (last_far, (2,)))
-
-        @pl.when(j == 8)
-        def _():
-            y_recv(9, FIRST)
-            y_issue(9, PASSED)
 
         permute(j, pl.ds(nb, 2 * nb), False)
         on(0, (first_far, (0, 1, 2, 3, VECTOR)))
@@ -393,9 +394,9 @@
         for done, new in ((2, (4,)), (3, (5,)), (4, (6,)), (5, (7,)), (7, (8, 9))):
             @pl.when(j == done)
             def _():
-                for n in new:
-                    y_issue(n, FIRST)
-                    y_issue(n, SECOND)
+                for k in (FIRST, SECOND):
+                    for n in new:
+                        y_issue(n, k)
 
         on(0, (start_third, (0, 1)))
         on(1, (start_third, (2, 3)))

time: 121 us -> 121 us (level)
  no operation moved by 1% of the time
where the time goes in v11:
time: 121 us
  Pallas kernels  121 us (100%)
    pallas_call x1, Pallas kernels, shards(): pl.pallas_call(body, out_shape=(jax.ShapeDtypeStruct((nb, nb), BF), jax.S...  119 us

profile of v11, /device:TPU:1, one launch (start us, length us, event | category | flops | bytes accessed | tf_op | source)
XLA Modules:
  0.0 121.3 jit_solution(10936255851460685407)
XLA Ops:
  0.6 118.8 %newton.1 = (bf16[512,512]{1,0:T(8,128)(2,1)}, f32[1,128]{1,0:T(1,128)}) custom-call(bf16[4,512,512]{2,1,0:T(8,128)(2,1)} %bitcast.4, s32[3,1,2048]{2,1,0:T(1,128)} %bitcast.5, s32[16,2048]{1,0:T(8,128)} %bpiv_hbm.1, bf16[4,128]{1,0:T(4,128)(2,1)} %bitcast.6), custom_call_target="tpu_custom_call" | custom-call | tf_op jit(solution)/shard_map/newton/pallas_call | solution.py:448
  119.5 1.9 %deliver.1 = (bf16[512,512]{1,0:T(8,128)(2,1)}, f32[1,128]{1,0:T(1,128)}) custom-call(bf16[512,512]{1,0:T(8,128)(2,1)} %get-tuple-element.6.block_ref, f32[1,128]{1,0:T(1,128)} %get-tuple-element.7.rhs_ref), custom_call_target="tpu_custom_call" | custom-call | tf_op jit(solution)/shard_map/deliver/pallas_call | solution.py:486
